TPU v7x, 256 devices: a whole 4x4x8 slice. The times are simulated.
256 devices in a mesh: blk: 64 (over y, z, x_hi), bin: 4 (over x_lo, core).
Axes of the slice: x: 4 (x_hi: 2, x_lo: 2; x = x_hi * 2 + x_lo), y: 4, z: 8, core: 2. Of those that a mesh axis runs over, the one named last changes fastest.
Arguments:
- spectrum: float32 [64, 8, 12, 512, 128], P('bin', None, None, 'blk'), may hold values from 0.05 to 2
- wind: float32 [8, 12, 128], replicated, may hold values from -12 to 12
- fall_speed: float32 [64], P('bin'), may hold values from 0.1 to 10
- collection: bfloat16 [64, 64, 64], P(None, None, 'bin'), may hold values from -0.09375 to 0.09375
- act_order: int32 [64, 8], P('blk'), may hold values from 0 to 7, each once within a row
- act_count: int32 [64], P('blk'), may hold values from 1 to 4, as said below
Outputs:
- updated: float32 [64, 8, 12, 512, 128], P('bin', None, None, 'blk')
Inputs may be any that keep to these rules, and one draw needn't show every extreme that they name: `act_order`: each row names every block row once; the active ones are its first act_count entries. `act_count`: some column holds exactly half of 8 active blocks.
All inputs are finite; a program needn't handle non-finite values.
Results may differ from a plain program's by a relative error of at most 0.0055.
Values may be sent and summed in bfloat16 or wider, within the bound.
A program may use at most 128 MiB of HBM per device.

v0:
```python
import jax
import jax.numpy as jnp
from jax import lax
from jax.sharding import PartitionSpec as P

weno_eps = 1e-06
courant = 0.04
time_step = 2.0


def padded_2(cells, sides, width):
    for axis, dim in sides:
        count = lax.axis_size(axis)
        ends = count - 1
        head = lax.slice_in_dim(cells, 0, width, axis=dim)
        tail = lax.slice_in_dim(cells, cells.shape[dim] - width, cells.shape[dim], axis=dim)
        cells = jnp.concatenate(
            [
                lax.ppermute(tail, axis, [(i, (i + 1) % count) for i in range(ends)]),
                cells,
                lax.ppermute(head, axis, [((i + 1) % count, i) for i in range(ends)]),
            ],
            axis=dim,
        )
    return cells


def reconstruct(first, second, third, fourth, fifth):
    cand_left = (2.0 * first - 7.0 * second + 11.0 * third) / 6.0
    cand_mid = (-second + 5.0 * third + 2.0 * fourth) / 6.0
    cand_right = (2.0 * third + 5.0 * fourth - fifth) / 6.0
    smooth_left = (
        13.0 / 12.0 * (first - 2.0 * second + third) ** 2
        + 0.25 * (first - 4.0 * second + 3.0 * third) ** 2
    )
    smooth_mid = 13.0 / 12.0 * (second - 2.0 * third + fourth) ** 2 + 0.25 * (second - fourth) ** 2
    smooth_right = (
        13.0 / 12.0 * (third - 2.0 * fourth + fifth) ** 2
        + 0.25 * (3.0 * third - 4.0 * fourth + fifth) ** 2
    )
    weight_left = 0.1 / (weno_eps + smooth_left) ** 2
    weight_mid = 0.6 / (weno_eps + smooth_mid) ** 2
    weight_right = 0.3 / (weno_eps + smooth_right) ** 2
    total = weight_left + weight_mid + weight_right
    return (weight_left * cand_left + weight_mid * cand_mid + weight_right * cand_right) / total


def face_terms(padded, width, wind):

    def window(offset):
        return lax.slice_in_dim(padded, offset, offset + width + 1, axis=3)

    upwind_pos = reconstruct(window(0), window(1), window(2), window(3), window(4))
    upwind_neg = reconstruct(window(5), window(4), window(3), window(2), window(1))
    speed = wind[None, :, :, None, :]
    return (speed, speed * upwind_pos, speed * upwind_neg)


def sediment(field, fall_speed):
    above = jnp.concatenate([field[:, :, 1:], jnp.zeros_like(field[:, :, :1])], axis=2)
    return field - courant * fall_speed[:, None, None, None, None] * (field - above)


def collide(spectra, table):
    count_in = spectra.shape[0]
    planes = spectra.shape[1] * spectra.shape[2]
    flat = spectra.reshape(count_in, planes, -1)
    out_bins = table.shape[1] // count_in

    def one_plane(index):
        cells = lax.dynamic_index_in_dim(flat, index, 1, keepdims=False)
        inner = lax.dot_general(
            table, cells, (((0,), (0,)), ((), ())), preferred_element_type=jnp.float32
        )
        inner = inner.astype(jnp.bfloat16).reshape(count_in, out_bins, -1)
        return jnp.einsum("ic,ikc->kc", cells, inner, preferred_element_type=jnp.float32)

    result = lax.map(one_plane, jnp.arange(planes, dtype=jnp.int32))
    return jnp.moveaxis(result, 0, 1).reshape((out_bins,) + spectra.shape[1:])


def local(spectrum, wind, fall_speed, collection, act_order, act_count):
    width = spectrum.shape[3]
    padded = padded_2(spectrum, (("blk", 3),), 3)
    speed, flux_pos, flux_neg = face_terms(padded, width, wind)
    flux = jnp.where(speed > 0, flux_pos, flux_neg)
    advected = spectrum - courant * (flux[:, :, :, 1:, :] - flux[:, :, :, :-1, :])
    settled = sediment(advected, fall_speed)
    slots = spectrum.shape[1]
    capacity = slots // 2
    order = act_order[0, :capacity]
    picked = jnp.take(settled, order, axis=1).astype(jnp.bfloat16)
    all_bins = collection.shape[0]
    whole = lax.all_gather(picked, "bin", axis=0, tiled=True)
    tendency = collide(whole, collection.reshape(all_bins, -1))
    entries = jnp.arange(capacity, dtype=jnp.int32)
    slot_ids = jnp.arange(slots, dtype=jnp.int32)
    chosen = jnp.logical_and(order[:, None] == slot_ids[None, :], (entries < act_count[0])[:, None])
    update = jnp.einsum("as,bazxy->bszxy", chosen.astype(jnp.float32), tendency)
    return settled + time_step * update


def solution(mesh):
    return jax.shard_map(
        local,
        mesh=mesh,
        in_specs=(
            P("bin", None, None, "blk", None),
            P(),
            P("bin"),
            P(None, None, "bin"),
            P("blk", None),
            P("blk"),
        ),
        out_specs=P("bin", None, None, "blk", None),
        check_vma=False,
    )
```

profile of v0, /device:TPU:1, one launch (start us, length us, event | category | flops | bytes accessed | tf_op | source)
XLA Modules:
  0.0 556.1 jit_solution(7151124852510900609)
XLA Ops:
  6.5 6.3 %fusion.39 = (f32[16,8,12,3,128]{4,3,2,1,0:T(4,128)S(1)}, f32[16,8,12,3,128]{4,3,2,1,0:T(4,128)S(1)}) fusion(f32[16,8,12,8,128]{4,3,2,1,0:T(8,128)} %param.8), kind=kLoop, calls=%fused_computation.63 | loop fusion | bytes 9437184 | tf_op jit(solution)/shard_map/slice | solution.py:16
  13.6 5.6 %collective-permute-start = (f32[16,8,12,3,128]{4,1,3,2,0:T(8,128)S(1)}, f32[16,8,12,3,128]{4,1,3,2,0:T(8,128)S(1)}, u32[]{:S(2)}, u32[]{:S(2)}) collective-permute-start(f32[16,8,12,3,128]{4,1,3,2,0:T(8,128)S(1)} %copy.47), channel_id=1, source_target_pairs={{0,4},{4,8},{8,12},{12,16},{16,20},{20,24},{24,28},{28,32},{32,36}... | collective-permute-start | bytes 7077896 | tf_op jit(solution)/shard_map/ppermute | solution.py:19
  19.2 2.2 copy.46
  22.8 96.8 %collective-permute-done = f32[16,8,12,3,128]{4,1,3,2,0:T(8,128)S(1)} collective-permute-done((f32[16,8,12,3,128]{4,1,3,2,0:T(8,128)S(1)}, f32[16,8,12,3,128]{4,1,3,2,0:T(8,128)S(1)}, u32[]{:S(2)}, u32[]{:S(2)}) %collective-permute-start) | collective-permute-done | bytes 2359328 | tf_op jit(solution)/shard_map/ppermute | solution.py:19
  119.7 7.7 %constant_dynamic-update-slice_fusion = (f32[16,8,12,11,128]{4,1,3,2,0:T(8,128)S(1)}, f32[16,8,12,11,128]{4,1,3,2,0:T(8,128)S(1)}) fusion(f32[16,8,12,11,128]{4,1,3,2,0:T(8,128)S(1)} %constant_dynamic-update-slice_fusion.1, f32[16,8,12,8,128]{4,3,2,1,0:T(8,128)} %param.8), kind=kLoop, calls=%fused_computation.46 | loop fusion | bytes 18874368 | tf_op jit(solution)/shard_map/concatenate | solution.py:17
  127.4 2.0 constant_dynamic-update-slice_fusion.2
  129.5 32.5 %multiply_select_fusion = f32[16,8,12,9,128]{4,1,3,2,0:T(8,128)} fusion(f32[16,8,12,11,128]{4,1,3,2,0:T(8,128)S(1)} %constant_dynamic-update-slice_fusion.2, f32[16,8,12,11,128]{4,1,3,2,0:T(8,128)S(1)} %get-tuple-element.48, f32[8,12,128]{2,0,1:T(8,128)S(1)} %copy-done.2, pred[8,12,128]{2,0,1:T(8,128)(4,1)S(1)} %broadcast_compare_fusion), kind=kLoop, calls=%fused_computation.8 | loop fusion | flops 224722944 | bytes 49606656 | tf_op jit(solution)/shard_map/jit(_where)/select_n | solution.py:86
  161.9 8.9 %fusion.27 = f32[16,8,12,8,128]{4,1,3,2,0:T(8,128)S(1)} fusion(f32[16,8,12,9,128]{4,1,3,2,0:T(8,128)} %multiply_select_fusion, f32[16,8,12,8,128]{4,3,2,1,0:T(8,128)S(1)} %bitcast.62), kind=kLoop, calls=%fused_computation.38 | loop fusion | flops 4718592 | bytes 25165824 | tf_op jit(solution)/shard_map/sub | solution.py:87
  171.8 2.4 multiply_subtract_fusion.2
  174.2 2.7 copy-done
  178.1 1.9 gather_fusion
  180.0 2.9 fusion.32
  184.2 70.7 %all-gather.2.cloned.1.call-done = bf16[64,4,12,8,128]{4,3,2,0,1:T(8,128)(2,1)} async-done(((bf16[16,4,12,8,128]{4,3,2,0,1:T(8,128)(2,1)}), bf16[64,4,12,8,128]{4,3,2,0,1:T(8,128)(2,1)}) %all-gather.2.cloned.1.call-update) | async-done | bytes 6291472 | tf_op jit(solution)/shard_map/all_gather | solution.py:94
  254.9 7.1 %copy.34 = bf16[64,4,12,8,128]{4,3,0,2,1:T(8,128)(2,1)} copy(bf16[64,4,12,8,128]{4,3,2,0,1:T(8,128)(2,1)} %all-gather.2.cloned.1.call-done) | data formatting | bytes 12582912 | tf_op jit(solution)/shard_map/while | solution.py:78
  262.0 10.3 %reshape.70 = bf16[64,48,1024]{2,0,1:T(8,128)(2,1)} reshape(bf16[64,4,12,8,128]{4,3,0,2,1:T(8,128)(2,1)} %copy.34) | data formatting | bytes 12582912 | tf_op jit(solution)/shard_map/while | solution.py:78
  272.3 268.3 %while.10 = (s32[]{:T(128)}, bf16[48,16,1024]{2,1,0:T(8,128)(2,1)S(1)}, s32[48]{0:T(128)S(1)}, bf16[64,48,1024]{2,0,1:T(8,128)(2,1)}, bf16[64,1024]{1,0:T(8,128)(2,1)S(1)}, /*index=5*/s32[]{:T(128)}, s32[]{:T(128)}, s32[]{:T(128)}) while((s32[]{:T(128)}, bf16[48,16,1024]{2,1,0:T(8,128)(2,1)S(1)}, s32[48]{0:T(128)S(1)}, ...), condition=%wide.region_1.2_spmd, body=%wide.region_0.1_spmd.sunk | while | flops 138461184 | bytes 5210255 | solution.py:78
  274.6 1.7 convolution_convert_fusion.2
  285.7 1.7 convolution_convert_fusion.2
  291.3 1.7 convolution_convert_fusion.2
  296.9 1.7 convolution_convert_fusion.2
  302.5 1.7 convolution_convert_fusion.2
  308.1 1.7 convolution_convert_fusion.2
  313.7 1.7 convolution_convert_fusion.2
  319.3 1.7 convolution_convert_fusion.2
  324.8 1.7 convolution_convert_fusion.2
  330.4 1.7 convolution_convert_fusion.2
  336.0 1.7 convolution_convert_fusion.2
  341.6 1.7 convolution_convert_fusion.2
  347.2 1.7 convolution_convert_fusion.2
  352.8 1.7 convolution_convert_fusion.2
  358.4 1.7 convolution_convert_fusion.2
  363.9 1.7 convolution_convert_fusion.2
  369.5 1.7 convolution_convert_fusion.2
  375.1 1.7 convolution_convert_fusion.2
  380.7 1.7 convolution_convert_fusion.2
  386.3 1.7 convolution_convert_fusion.2
  391.9 1.7 convolution_convert_fusion.2
  397.5 1.7 convolution_convert_fusion.2
  403.0 1.7 convolution_convert_fusion.2
  408.6 1.7 convolution_convert_fusion.2
  414.2 1.7 convolution_convert_fusion.2
  419.8 1.7 convolution_convert_fusion.2
  425.4 1.7 convolution_convert_fusion.2
  431.0 1.7 convolution_convert_fusion.2
  436.6 1.7 convolution_convert_fusion.2
  442.1 1.7 convolution_convert_fusion.2
  447.7 1.7 convolution_convert_fusion.2
  453.3 1.7 convolution_convert_fusion.2
  458.9 1.7 convolution_convert_fusion.2
  464.5 1.7 convolution_convert_fusion.2
  470.1 1.7 convolution_convert_fusion.2
  475.6 1.7 convolution_convert_fusion.2
  481.2 1.7 convolution_convert_fusion.2
  486.8 1.7 convolution_convert_fusion.2
  492.4 1.7 convolution_convert_fusion.2
  498.0 1.7 convolution_convert_fusion.2
  503.6 1.7 convolution_convert_fusion.2
  509.2 1.7 convolution_convert_fusion.2
  514.7 1.7 convolution_convert_fusion.2
  520.3 1.7 convolution_convert_fusion.2
  531.5 1.7 convolution_convert_fusion.2
  537.1 1.7 convolution_convert_fusion.2
  541.1 4.4 bitcast_add_fusion
  545.5 3.8 copy.26
  (228 shorter events, 115.2 us)
Async XLA Ops:
  6.5 248.3 %all-gather.2.cloned.1.call-start = ((), (), s32[]{:S(2)}) async-start(), calls=%async_computation | async-start | bytes 7864320 | tf_op jit(solution)/shard_map/all_gather | solution.py:94
  12.8 9.9 %copy-start.4 = (s32[1,8]{1,0:T(1,128)S(1)}, s32[1,8]{1,0:T(1,128)}, u32[]{:S(2)}) copy-start(s32[1,8]{1,0:T(1,128)} %param.12) | copy-start | bytes 100
  12.8 9.9 %copy-start.3 = (f32[16]{0:T(128)S(1)}, f32[16]{0:T(128)}, u32[]{:S(2)}) copy-start(f32[16]{0:T(128)} %param.10) | copy-start | bytes 196
  12.8 9.9 %copy-start.2 = (f32[8,12,128]{2,0,1:T(8,128)S(1)}, f32[8,12,128]{2,0,1:T(8,128)}, u32[]{:S(2)}) copy-start(f32[8,12,128]{2,0,1:T(8,128)} %param.9) | copy-start | bytes 147460
  13.6 105.9 %collective-permute-start = (f32[16,8,12,3,128]{4,1,3,2,0:T(8,128)S(1)}, f32[16,8,12,3,128]{4,1,3,2,0:T(8,128)S(1)}, u32[]{:S(2)}, u32[]{:S(2)}) collective-permute-start(f32[16,8,12,3,128]{4,1,3,2,0:T(8,128)S(1)} %copy.47), channel_id=1, source_target_pairs={{0,4},{4,8},{8,12},{12,16},{16,20},{20,24},{24,28},{28,32},{32,36}... | collective-permute-start | bytes 7077896 | tf_op jit(solution)/shard_map/ppermute | solution.py:19
  21.4 106.0 %collective-permute-start.1 = (f32[16,8,12,3,128]{4,1,3,2,0:T(8,128)}, f32[16,8,12,3,128]{4,1,3,2,0:T(8,128)}, u32[]{:S(2)}, u32[]{:S(2)}) collective-permute-start(f32[16,8,12,3,128]{4,1,3,2,0:T(8,128)} %copy.46), channel_id=1, source_target_pairs={{4,0},{8,4},{12,8},{16,12},{20,16},{24,20},{28,24},{32,28},{36,32}... | collective-permute-start | bytes 7077896 | tf_op jit(solution)/shard_map/ppermute | solution.py:21
  127.4 34.5 %slice-start = ((s8[6291456]{0:T(1024)(128)(4,1)}), s8[4194304]{0:T(1024)(128)(4,1)S(1)}, s32[]{:S(2)}) async-start(s8[6291456]{0:T(1024)(128)(4,1)} %bitcast.61), calls=%async_computation.1 | async-start | bytes 8388608
  129.4 32.5 %slice-start.1 = ((s8[6291456]{0:T(1024)(128)(4,1)}), s8[2097152]{0:T(1024)(128)(4,1)S(1)}, s32[]{:S(2)}) async-start(s8[6291456]{0:T(1024)(128)(4,1)} %bitcast.61), calls=%async_computation.2 | async-start | bytes 4194304
  174.2 2.7 copy-start
  176.9 6.1 %copy-start.1 = (bf16[64,64,16]{1,2,0:T(8,128)(2,1)S(1)}, bf16[64,64,16]{1,2,0:T(8,128)(2,1)}, u32[]{:S(2)}) copy-start(bf16[64,64,16]{1,2,0:T(8,128)(2,1)} %param.11) | copy-start | bytes 393220
Sparse Core Ops, SparseCore 0:
  183.1 71.7 all-gather.1
where the time goes:
time: 559 us; the launch traced here: 556 us
  waiting for transfers between devices  167 us (30%)
  other arithmetic  125 us (22%)
  matrix products  84 us (15%)
  loops' own time  82.2 us (15%)
  local copies, waits for them, and re-layouts  76.2 us (14%)
  between operations  14.3 us (3%)
  starting transfers between devices  6.91 us (1%)
    ppermute x1, waiting for transfers between devices, padded_2(): lax.ppermute(tail, axis, [(i, (i + 1) % count) for i in range(ends)])  96.8 us
    another operation x1, loops' own time, collide(): result = lax.map(one_plane, jnp.arange(planes, dtype=jnp.int32))  82.2 us
    dot_general x48, matrix products, one_plane(): lax.dot_general(table, cells, (((0,), (0,)), ((), ())), preferred_element...  79.6 us
    all_gather x1, waiting for transfers between devices, local(): whole = lax.all_gather(picked, 'bin', axis=0, tiled=True)  70.7 us
    while x48, other arithmetic  44.6 us
    dot_general x48, other arithmetic, one_plane(): jnp.einsum('ic,ikc->kc', cells, inner, preferred_element_type=jnp.float32)  33.7 us
    select_n x1, other arithmetic, local(): flux = jnp.where(speed > 0, flux_pos, flux_neg)  32.5 us
    dynamic_slice x48, local copies, waits for them, and re-layouts, collide(): result = lax.map(one_plane, jnp.arange(planes, dtype=jnp.int32))  27.8 us
  transfers between devices with their start and end apart: 3, of which 2 were waited for; matrix products, arithmetic and copies ran while one was open for 2% of the time, Pallas kernels for 0%

commit v1 on v0

v1 whole, which is shorter than its diff:
```python
import functools

import jax
import jax.numpy as jnp
from jax import lax
from jax.experimental import pallas as pl
from jax.experimental.pallas import tpu as pltpu
from jax.sharding import PartitionSpec as P

courant = 0.04
time_step = 2.0
f32 = jnp.float32
bf16 = jnp.bfloat16


def pieces(ref):
    return ref.reshape(ref.shape[0] * ref.shape[1] * ref.shape[2] * ref.shape[3], ref.shape[4])


def edges_body(spec_ref, head_ref, tail_ref):
    bins, _, nz, bx, _ = spec_ref.shape
    flat = pieces(spec_ref)

    def level(z, carry):
        for x in range(3):
            for first, out in ((0, head_ref), (bx - 3, tail_ref)):
                rows = flat[pl.ds(z * bx + first + x, bins, stride=nz * bx), :]
                out[0, z, x] = rows.astype(bf16)
        return carry

    lax.fori_loop(0, nz, level, 0)


def advect_cells(p, pos, half_cw, sixth_cw):
    u = [jnp.where(pos, p[k], p[13 - k]) for k in range(13)]
    d = [u[k + 1] - u[k] for k in range(12)]
    s, ss, first, left, mid, right = {}, {}, {}, {}, {}, {}
    for j in range(1, 12):
        s[j] = d[j] - d[j - 1]
        ss[j] = s[j] + s[j]
        t = d[j] + d[j - 1]
        h = s[j] * s[j] * (13.0 / 3.0) + 4e-6
        if j <= 9:
            first[j] = t + ss[j]
            b = h + first[j] * first[j]
            left[j] = b * b
        if 2 <= j <= 10:
            b = h + t * t
            mid[j] = b * b
        if j >= 3:
            t = t - ss[j]
            b = h + t * t
            right[j] = b * b
    r = []
    for g in range(9):
        a, b, c = left[g + 1], mid[g + 2], right[g + 3]
        wl = b * c
        a3 = a * 3.0
        wm = a3 * (c + c)
        wr = a3 * b
        num = wl * ss[g + 1] + wm * ss[g + 2] + wr * (ss[g + 2] + (s[g + 2] - s[g + 3]))
        r.append(num / (wl + wm + wr))
    moved = [u[m + 3] - (half_cw * first[m + 2] + sixth_cw * (r[m + 1] - r[m])) for m in range(8)]
    return [jnp.where(pos, moved[i], moved[7 - i]) for i in range(8)]


def transport_body(order_ref, spec_ref, left_ref, right_ref, wind_ref, fall_ref, out_ref, pick_ref):
    bins, _, nz, bx, by = spec_ref.shape
    flat, flat_out = pieces(spec_ref), pieces(out_ref)
    active = pl.program_id(0) < pl.num_programs(0) // 2

    for half in range(bins // 8):
        first = half * 8
        fall = fall_ref[first : first + 8, :]

        def level(step, above, first=first, fall=fall):
            z = nz - 1 - step
            speed = jnp.broadcast_to(wind_ref[0, pl.ds(z, 1), :], (8, by))
            pos = speed > 0
            cw = courant * jnp.abs(speed)
            own = [flat[pl.ds(first * nz * bx + z * bx + x, 8, stride=nz * bx), :] for x in range(bx)]
            head = [left_ref[0, z, x, first : first + 8, :].astype(f32) for x in range(3)]
            tail = [right_ref[0, z, x, first : first + 8, :].astype(f32) for x in range(3)]
            adv = advect_cells(head + own + tail, pos, cw * 0.5, cw * (1.0 / 6.0))
            settled = [adv[x] - fall * (adv[x] - above[x]) for x in range(bx)]
            for x in range(bx):
                flat_out[pl.ds(first * nz * bx + z * bx + x, 8, stride=nz * bx), :] = settled[x]

            @pl.when(active)
            def _():
                for x in range(bx):
                    pick_ref[0, z, x, first : first + 8, :] = settled[x].astype(bf16)

            return tuple(adv)

        lax.fori_loop(0, nz, level, tuple(jnp.zeros((8, by), f32) for _ in range(bx)))


def collect_body(got_ref, table_ref, out_ref, cells_ref, prod_ref):
    bx, by = got_ref.shape[3], got_ref.shape[5]

    def pair(step, carry):
        for part in range(2):
            x = step * 2 + part
            lanes = slice(part * by, (part + 1) * by)
            cells = [got_ref[q, 0, 0, x] for q in range(4)]
            for q in range(4):
                cells_ref[q * 16 : q * 16 + 16, :] = cells[q].astype(f32)
            row = 0
            for i in range(64):
                one = jnp.broadcast_to(cells_ref[i : i + 1, :], (16, by)).astype(bf16)
                for q in range(i // 16, 4):
                    prod_ref[row : row + 16, lanes] = one * cells[q]
                    row += 16
        total = jnp.dot(table_ref[...], prod_ref[...], preferred_element_type=f32).astype(bf16)
        for part in range(2):
            for q in range(4):
                out_ref[q, 0, 0, step * 2 + part] = total[q * 16 : q * 16 + 16, part * by : (part + 1) * by]
        return carry

    lax.fori_loop(0, bx // 2, pair, 0)


def update_body(order_ref, count_ref, settled_ref, tend_ref, out_ref):
    bins, _, nz, bx, by = settled_ref.shape
    flat, flat_out = pieces(settled_ref), pieces(out_ref)
    on = jnp.full((bins, by), pl.program_id(0), jnp.int32) < count_ref[0]

    def level(z, carry):
        for x in range(bx):
            where = pl.ds(z * bx + x, bins, stride=nz * bx)
            add = tend_ref[0, z, x].astype(f32) * time_step
            flat_out[where, :] = flat[where, :] + jnp.where(on, add, 0.0)
        return carry

    lax.fori_loop(0, nz, level, 0)


def pair_table(collection):
    t = jnp.transpose(collection, (2, 1, 0)).astype(f32)
    both = (t + jnp.transpose(t, (0, 2, 1))).astype(bf16)
    t = t.astype(bf16)
    parts = []
    for q in range(4):
        lo, hi = q * 16, q * 16 + 16
        rows = jnp.concatenate([t[:, lo:hi, lo:hi], both[:, lo:hi, hi:]], axis=2)
        parts.append(rows.reshape(64, -1))
    return jnp.concatenate(parts, axis=1)


def local(spectrum, wind, fall_speed, collection, act_order, act_count):
    bins, slots, nz, bx, by = spectrum.shape
    count = lax.axis_size("blk")
    order = act_order[0]
    half = slots // 2
    block = (bins, 1, nz, bx, by)
    side = (1, nz, 3, bins, by)
    side_shape = jax.ShapeDtypeStruct((slots, nz, 3, bins, by), bf16)

    heads, tails = pl.pallas_call(
        edges_body,
        grid=(slots,),
        in_specs=[pl.BlockSpec(block, lambda r: (0, r, 0, 0, 0))],
        out_specs=[pl.BlockSpec(side, lambda r: (r, 0, 0, 0, 0))] * 2,
        out_shape=[side_shape] * 2,
    )(spectrum)
    left = lax.ppermute(tails, "blk", [(i, i + 1) for i in range(count - 1)])
    right = lax.ppermute(heads, "blk", [(i + 1, i) for i in range(count - 1)])

    whole = lax.all_gather(collection, "bin", axis=2, tiled=True)
    table = pair_table(whole)

    fall = jnp.broadcast_to((courant * fall_speed)[:, None], (bins, by))
    settled, picked = pl.pallas_call(
        transport_body,
        grid_spec=pltpu.PrefetchScalarGridSpec(
            num_scalar_prefetch=1,
            grid=(slots,),
            in_specs=[
                pl.BlockSpec(block, lambda g, o: (0, o[g], 0, 0, 0)),
                pl.BlockSpec(side, lambda g, o: (o[g], 0, 0, 0, 0)),
                pl.BlockSpec(side, lambda g, o: (o[g], 0, 0, 0, 0)),
                pl.BlockSpec((1, nz, by), lambda g, o: (o[g], 0, 0)),
                pl.BlockSpec((bins, by), lambda g, o: (0, 0)),
            ],
            out_specs=[
                pl.BlockSpec(block, lambda g, o: (0, o[g], 0, 0, 0)),
                pl.BlockSpec((1, nz, bx, bins, by), lambda g, o: (jnp.minimum(g, 3), 0, 0, 0, 0)),
            ],
        ),
        out_shape=[
            jax.ShapeDtypeStruct(spectrum.shape, f32),
            jax.ShapeDtypeStruct((half, nz, bx, bins, by), bf16),
        ],
    )(order, spectrum, left, right, wind, fall)

    parts = 4
    share = nz // parts
    send = picked.reshape(half, parts, share, bx, bins, by)
    got = lax.all_to_all(jnp.moveaxis(send, 1, 0), "bin", 0, 0)
    tile = (parts, 1, 1, bx, bins, by)
    where = lambda a, z: (0, a, z, 0, 0, 0)
    tend = pl.pallas_call(
        collect_body,
        grid=(half, share),
        in_specs=[pl.BlockSpec(tile, where), pl.BlockSpec(table.shape, lambda a, z: (0, 0))],
        out_specs=pl.BlockSpec(tile, where),
        out_shape=jax.ShapeDtypeStruct((parts, half, share, bx, bins, by), bf16),
        scratch_shapes=[pltpu.VMEM((64, by), f32), pltpu.VMEM((2560, 2 * by), bf16)],
    )(got, table)
    back = lax.all_to_all(tend, "bin", 0, 0)
    back = jnp.moveaxis(back, 0, 1).reshape(half, nz, bx, bins, by)

    return pl.pallas_call(
        update_body,
        grid_spec=pltpu.PrefetchScalarGridSpec(
            num_scalar_prefetch=2,
            grid=(half,),
            in_specs=[
                pl.BlockSpec(block, lambda a, o, c: (0, o[a], 0, 0, 0)),
                pl.BlockSpec((1, nz, bx, bins, by), lambda a, o, c: (a, 0, 0, 0, 0)),
            ],
            out_specs=pl.BlockSpec(block, lambda a, o, c: (0, o[a], 0, 0, 0)),
        ),
        out_shape=jax.ShapeDtypeStruct(spectrum.shape, f32),
        input_output_aliases={2: 0},
    )(order, act_count, settled, back)


def solution(mesh):
    return jax.shard_map(
        local,
        mesh=mesh,
        in_specs=(
            P("bin", None, None, "blk", None),
            P(),
            P("bin"),
            P(None, None, "bin"),
            P("blk", None),
            P("blk"),
        ),
        out_specs=P("bin", None, None, "blk", None),
        check_vma=False,
    )
```

time: 559 us -> 182 us (0.33)
  waiting for transfers between devices: 167 us -> 34.2 us
  other arithmetic: 125 us -> 1.6 us
  matrix products: 84 us -> 0 us
  loops' own time: 82.2 us -> 0 us
  local copies, waits for them, and re-layouts: 76.2 us -> 10.3 us
  Pallas kernels: 0 us -> 59.6 us
  blocking collectives: 0 us -> 57 us
  between operations: 14.3 us -> 0.83 us
  starting transfers between devices: 6.91 us -> 15.7 us
    ppermute x2, waiting for transfers between devices: 96.8 us -> 0.01 us  [the longest x1 0.01 us: local(): right = lax.ppermute(heads, 'blk', [(i + 1, i) for i in range(count - 1)])]
    dot_general x49 -> x0, matrix products: 84 us -> none  [the longest x48 79.6 us: one_plane(): lax.dot_general(table, cells, (((0,), (0,)), ((), ())), preferred_element...]
    another operation x1 -> x0, loops' own time: 82.2 us -> none  [collide(): result = lax.map(one_plane, jnp.arange(planes, dtype=jnp.int32))]
    all_gather x1 -> x0, waiting for transfers between devices: 70.7 us -> none  [local(): whole = lax.all_gather(picked, 'bin', axis=0, tiled=True)]
    pallas_call x0 -> x4, Pallas kernels: none -> 59.6 us  [the longest x1 22.6 us: local(): pl.pallas_call(transport_body, grid_spec=pltpu.PrefetchScalarGridSpec(num...]
    all_gather x0 -> x1, blocking collectives: none -> 57 us  [local(): whole = lax.all_gather(collection, 'bin', axis=2, tiled=True)]
    while x48 -> x0, other arithmetic: 44.6 us -> none
    all_to_all x0 -> x2, waiting for transfers between devices: none -> 34.2 us  [the longest x1 18.6 us: local(): back = lax.all_to_all(tend, 'bin', 0, 0)]
  transfers between devices with their start and end apart: 3 -> 4, of which waited for: 2 -> 2; matrix products, arithmetic and copies ran while one was open for 2% -> 4% of each run, Pallas kernels for 0% -> 0%
where the time goes in v1:
time: 182 us; the launch traced here: 179 us
  Pallas kernels  59.6 us (33%)
  blocking collectives  57 us (31%)
  waiting for transfers between devices  34.2 us (19%)
  starting transfers between devices  15.7 us (9%)
  local copies, waits for them, and re-layouts  10.3 us (6%)
    all_gather x1, blocking collectives, local(): whole = lax.all_gather(collection, 'bin', axis=2, tiled=True)  57 us
    pallas_call x1, Pallas kernels, local(): pl.pallas_call(transport_body, grid_spec=pltpu.PrefetchScalarGridSpec(num...  22.6 us
    pallas_call x1, Pallas kernels, local(): pl.pallas_call(collect_body, grid=(half, share), in_specs=[pl.BlockSpec(t...  21.7 us
    all_to_all x1, waiting for transfers between devices, local(): back = lax.all_to_all(tend, 'bin', 0, 0)  18.6 us
    all_to_all x1, waiting for transfers between devices, local(): got = lax.all_to_all(jnp.moveaxis(send, 1, 0), 'bin', 0, 0)  15.6 us
    pallas_call x1, Pallas kernels, local(): pl.pallas_call(edges_body, grid=(slots,), in_specs=[pl.BlockSpec(block, l...  7.99 us
    pallas_call x1, Pallas kernels, local(): pl.pallas_call(update_body, grid_spec=pltpu.PrefetchScalarGridSpec(num_sc...  7.37 us
    ppermute x1, starting transfers between devices, local(): left = lax.ppermute(tails, 'blk', [(i, i + 1) for i in range(count - 1)])  5.54 us
  transfers between devices with their start and end apart: 4, of which 2 were waited for; matrix products, arithmetic and copies ran while one was open for 4% of the time, Pallas kernels for 0%

profile of v1, /device:TPU:1, one launch (start us, length us, event | category | flops | bytes accessed | tf_op | source)
XLA Modules:
  0.0 179.3 jit_solution(16807709952567755421)
XLA Ops:
  0.0 0.0 copy-start.2
  0.0 0.0 copy-start.1
  0.0 8.0 %shard_map.64 = (bf16[8,12,3,16,128]{4,3,2,1,0:T(8,128)(2,1)}, bf16[8,12,3,16,128]{4,3,2,1,0:T(8,128)(2,1)}) custom-call(f32[16,8,12,8,128]{4,3,2,1,0:T(8,128)} %spec_ref.3), custom_call_target="tpu_custom_call" | custom-call | tf_op jit(solution)/shard_map/pallas_call | solution.py:160
  8.0 5.5 %collective-permute-start = (bf16[8,12,3,16,128]{4,3,2,1,0:T(8,128)(2,1)}, bf16[8,12,3,16,128]{4,3,2,1,0:T(8,128)(2,1)S(1)}, u32[]{:S(2)}, u32[]{:S(2)}) collective-permute-start(bf16[8,12,3,16,128]{4,3,2,1,0:T(8,128)(2,1)} %get-tuple-element.9), channel_id=1, source_target_pairs={{0,4},{4,8},{8,12},{12,16},{16,20},{20,24},{24,28},{28,32},{32,36}... | collective-permute-start | bytes 3538952 | tf_op jit(solution)/shard_map/ppermute | solution.py:167
  13.5 1.3 collective-permute-start.1
  14.8 0.0 copy-done.2
  14.8 0.6 copy.15.wind_ref
  15.5 0.0 copy-done.1
  15.5 0.0 copy-start.3
  15.5 57.0 %all_gather.3 = bf16[64,64,64]{1,2,0:T(8,128)(2,1)S(1)} all-gather(bf16[64,64,16]{1,2,0:T(8,128)(2,1)S(1)} %copy-done.1), channel_id=1, replica_groups=mesh['blk'=64,'bin'=4] {'bin'}, dimensions={2}, use_global_device_ids=true | all-gather | bytes 655360 | tf_op jit(solution)/shard_map/all_gather | solution.py:170
  72.5 2.2 %copy.17 = bf16[64,64,64]{0,2,1:T(8,128)(2,1)S(1)} copy(bf16[64,64,64]{1,2,0:T(8,128)(2,1)S(1)} %all_gather.3) | data formatting | bytes 1048576 | tf_op jit(solution)/shard_map/all_gather | solution.py:170
  74.7 0.0 copy-done.3
  74.8 0.0 collective-permute-done.left_ref
  74.8 0.0 copy-start
  74.8 0.0 collective-permute-done.1.right_ref
  74.8 0.8 broadcast_in_dim.2.fall_ref
  75.6 0.2 copy-done
  75.8 22.6 %shard_map.65 = (f32[16,8,12,8,128]{4,3,2,1,0:T(8,128)}, bf16[4,12,8,16,128]{4,3,2,1,0:T(8,128)(2,1)}) custom-call(s32[8]{0:T(128)} %bitcast.22, f32[16,8,12,8,128]{4,3,2,1,0:T(8,128)} %spec_ref.3, bf16[8,12,3,16,128]{4,3,2,1,0:T(8,128)(2,1)} %copy-done, bf16[8,12,3,16,128]{4,3,2,1,0:T(8,128)(2,1)} %collective-permute-done.1.right_ref, ...), custom_call_target="tpu_custom_call" | custom-call | tf_op jit(solution)/shard_map/pallas_call | solution.py:174
  98.4 3.0 %copy.26 = bf16[4,4,3,8,16,128]{5,4,3,2,0,1:T(8,128)(2,1)} copy(bf16[4,4,3,8,16,128]{5,4,3,2,1,0:T(8,128)(2,1)} %bitcast.19) | data formatting | bytes 3145728 | tf_op jit(solution)/shard_map/reshape | solution.py:199
  101.4 4.5 %all-to-all-start = ((bf16[4,4,3,8,16,128]{5,4,3,2,1,0:T(8,128)(2,1)}), bf16[4,4,3,8,16,128]{5,4,3,2,1,0:T(8,128)(2,1)}, u32[]{:S(2)}, u32[]{:S(2)}) async-start(bf16[4,4,3,8,16,128]{5,4,3,2,1,0:T(8,128)(2,1)} %bitcast.16), calls=%async_computation | async-start | bytes 3145728 | tf_op jit(solution)/shard_map/all_to_all | solution.py:200
  105.9 0.4 fusion
  106.2 0.1 slice.33
  106.4 0.1 slice.31
  106.5 0.1 slice.29
  106.7 0.3 fusion.1
  107.0 0.1 copy.21
  107.1 0.1 copy.23
  107.2 0.2 pad_maximum_fusion.3
  107.4 0.1 copy.20
  107.5 0.1 copy.22
  107.7 0.2 pad_maximum_fusion.2
  107.8 0.2 copy.19
  108.0 0.3 reshape.21
  108.3 0.2 pad_maximum_fusion.1
  108.4 0.2 copy.18
  108.6 0.2 reshape.20
  108.8 0.8 pad_maximum_fusion.table_ref
  109.5 15.6 %all-to-all-done.got_ref = bf16[4,4,3,8,16,128]{5,4,3,2,1,0:T(8,128)(2,1)} async-done(((bf16[4,4,3,8,16,128]{5,4,3,2,1,0:T(8,128)(2,1)}), bf16[4,4,3,8,16,128]{5,4,3,2,1,0:T(8,128)(2,1)}, u32[]{:S(2)}, u32[]{:S(2)}) %all-to-all-start) | async-done | bytes 1572896 | tf_op jit(solution)/shard_map/all_to_all | solution.py:200
  125.2 21.7 %shard_map.66 = bf16[4,4,3,8,16,128]{5,4,3,2,1,0:T(8,128)(2,1)} custom-call(bf16[4,4,3,8,16,128]{5,4,3,2,1,0:T(8,128)(2,1)} %all-to-all-done.got_ref, bf16[64,2560]{1,0:T(8,128)(2,1)} %pad_maximum_fusion.table_ref), custom_call_target="tpu_custom_call" | custom-call | tf_op jit(solution)/shard_map/pallas_call | solution.py:203
  146.9 4.4 %all-to-all-start.1 = ((bf16[4,4,3,8,16,128]{5,4,3,2,1,0:T(8,128)(2,1)}), bf16[4,4,3,8,16,128]{5,4,3,2,1,0:T(8,128)(2,1)S(1)}, u32[]{:S(2)}, u32[]{:S(2)}) async-start(bf16[4,4,3,8,16,128]{5,4,3,2,1,0:T(8,128)(2,1)} %shard_map.66), calls=%async_computation.1 | async-start | bytes 3145728 | tf_op jit(solution)/shard_map/all_to_all | solution.py:211
  151.9 18.6 %all-to-all-done.1 = bf16[4,4,3,8,16,128]{5,4,3,2,1,0:T(8,128)(2,1)S(1)} async-done(((bf16[4,4,3,8,16,128]{5,4,3,2,1,0:T(8,128)(2,1)}), bf16[4,4,3,8,16,128]{5,4,3,2,1,0:T(8,128)(2,1)S(1)}, u32[]{:S(2)}, u32[]{:S(2)}) %all-to-all-start.1) | async-done | bytes 1572896 | tf_op jit(solution)/shard_map/all_to_all | solution.py:211
  170.5 1.4 copy.24
  171.9 7.4 %shard_map.67 = f32[16,8,12,8,128]{4,3,2,1,0:T(8,128)} custom-call(s32[8]{0:T(128)} %bitcast.23, s32[1]{0:T(128)S(6)} %copy.28.count_ref, f32[16,8,12,8,128]{4,3,2,1,0:T(8,128)} %get-tuple-element.11.settled_ref, bf16[4,12,8,16,128]{4,3,2,1,0:T(8,128)(2,1)} %bitcast.18), custom_call_target="tpu_custom_call", output_to_operand_aliasing={{}: (2, {})} | custom-call | tf_op jit(solution)/shard_map/pallas_call | solution.py:214
  (1 shorter events, 0.0 us)
Async XLA Ops:
  0.0 14.8 %copy-start.2 = (f32[8,12,128]{2,0,1:T(8,128)S(1)}, f32[8,12,128]{2,0,1:T(8,128)}, u32[]{:S(2)}) copy-start(f32[8,12,128]{2,0,1:T(8,128)} %param.7) | copy-start | bytes 147460
  0.0 15.5 %copy-start.1 = (bf16[64,64,16]{1,2,0:T(8,128)(2,1)S(1)}, bf16[64,64,16]{1,2,0:T(8,128)(2,1)}, u32[]{:S(2)}) copy-start(bf16[64,64,16]{1,2,0:T(8,128)(2,1)} %param.9) | copy-start | bytes 393220
  8.0 66.8 %collective-permute-start = (bf16[8,12,3,16,128]{4,3,2,1,0:T(8,128)(2,1)}, bf16[8,12,3,16,128]{4,3,2,1,0:T(8,128)(2,1)S(1)}, u32[]{:S(2)}, u32[]{:S(2)}) collective-permute-start(bf16[8,12,3,16,128]{4,3,2,1,0:T(8,128)(2,1)} %get-tuple-element.9), channel_id=1, source_target_pairs={{0,4},{4,8},{8,12},{12,16},{16,20},{20,24},{24,28},{28,32},{32,36}... | collective-permute-start | bytes 3538952 | tf_op jit(solution)/shard_map/ppermute | solution.py:167
  13.5 61.3 %collective-permute-start.1 = (bf16[8,12,3,16,128]{4,3,2,1,0:T(8,128)(2,1)}, bf16[8,12,3,16,128]{4,3,2,1,0:T(8,128)(2,1)}, u32[]{:S(2)}, u32[]{:S(2)}) collective-permute-start(bf16[8,12,3,16,128]{4,3,2,1,0:T(8,128)(2,1)} %get-tuple-element.10), channel_id=1, source_target_pairs={{4,0},{8,4},{12,8},{16,12},{20,16},{24,20},{28,24},{32,28},{36,32}... | collective-permute-start | bytes 3538952 | tf_op jit(solution)/shard_map/ppermute | solution.py:168
  15.5 59.3 %copy-start.3 = (f32[16]{0:T(128)S(1)}, f32[16]{0:T(128)}, u32[]{:S(2)}) copy-start(f32[16]{0:T(128)} %param.8) | copy-start | bytes 196
  74.8 1.0 copy-start
  101.4 23.8 %all-to-all-start = ((bf16[4,4,3,8,16,128]{5,4,3,2,1,0:T(8,128)(2,1)}), bf16[4,4,3,8,16,128]{5,4,3,2,1,0:T(8,128)(2,1)}, u32[]{:S(2)}, u32[]{:S(2)}) async-start(bf16[4,4,3,8,16,128]{5,4,3,2,1,0:T(8,128)(2,1)} %bitcast.16), calls=%async_computation | async-start | bytes 3145728 | tf_op jit(solution)/shard_map/all_to_all | solution.py:200
  146.9 23.6 %all-to-all-start.1 = ((bf16[4,4,3,8,16,128]{5,4,3,2,1,0:T(8,128)(2,1)}), bf16[4,4,3,8,16,128]{5,4,3,2,1,0:T(8,128)(2,1)S(1)}, u32[]{:S(2)}, u32[]{:S(2)}) async-start(bf16[4,4,3,8,16,128]{5,4,3,2,1,0:T(8,128)(2,1)} %shard_map.66), calls=%async_computation.1 | async-start | bytes 3145728 | tf_op jit(solution)/shard_map/all_to_all | solution.py:211

commit v2 on v1

v2 whole, which is shorter than its diff:
```python
import jax
import jax.numpy as jnp
from jax import lax
from jax.experimental import pallas as pl
from jax.experimental.pallas import tpu as pltpu
from jax.sharding import PartitionSpec as P

courant = 0.04
time_step = 2.0
f32 = jnp.float32
bf16 = jnp.bfloat16
MESH = pl.DeviceIdType.MESH


def pieces(ref):
    return ref.reshape(ref.shape[0] * ref.shape[1] * ref.shape[2] * ref.shape[3], ref.shape[4])


def advect_cells(p, pos, half_cw, sixth_cw):
    u = [jnp.where(pos, p[k], p[13 - k]) for k in range(13)]
    d = [u[k + 1] - u[k] for k in range(12)]
    s, ss, first, left, mid, right = {}, {}, {}, {}, {}, {}
    for j in range(1, 12):
        s[j] = d[j] - d[j - 1]
        ss[j] = s[j] + s[j]
        t = d[j] + d[j - 1]
        h = s[j] * s[j] * (13.0 / 3.0) + 4e-6
        if j <= 9:
            first[j] = t + ss[j]
            b = h + first[j] * first[j]
            left[j] = b * b
        if 2 <= j <= 10:
            b = h + t * t
            mid[j] = b * b
        if j >= 3:
            t = t - ss[j]
            b = h + t * t
            right[j] = b * b
    r = []
    for g in range(9):
        a, b, c = left[g + 1], mid[g + 2], right[g + 3]
        wl = b * c
        a3 = a * 3.0
        wm = a3 * (c + c)
        wr = a3 * b
        num = wl * ss[g + 1] + wm * ss[g + 2] + wr * (ss[g + 2] + (s[g + 2] - s[g + 3]))
        r.append(num / (wl + wm + wr))
    moved = [u[m + 3] - (half_cw * first[m + 2] + sixth_cw * (r[m + 1] - r[m])) for m in range(8)]
    return [jnp.where(pos, moved[i], moved[7 - i]) for i in range(8)]


def step_body(
    order_ref, left_order_ref, right_order_ref, spec_ref, wind_ref, fall_ref, own_table_ref,
    settled_out, back_out,
    table_ref, heads, tails, from_left, from_right, settled_ref, picks, got, tends, cells_ref, prod_ref,
    halo_sent, halo_got, pick_sent, pick_got, back_sent, back_got, table_sent, table_got, out_sem, own_sem,
):
    bins, slots, nz, bx, by = spec_ref.shape
    half = slots // 2
    flat = pieces(spec_ref)
    blk, bin_ = lax.axis_index("blk"), lax.axis_index("bin")
    n_blk, n_bin = lax.axis_size("blk"), lax.axis_size("bin")
    share = nz // n_bin
    last = n_blk - 1
    right, left = lax.rem(blk + 1, n_blk), lax.rem(blk + last, n_blk)
    peers = [lax.rem(bin_ + k, n_bin) for k in range(1, n_bin)]

    barrier = pltpu.get_barrier_semaphore()
    for side in (left, right):
        pl.semaphore_signal(barrier, inc=1, device_id={"blk": side}, device_id_type=MESH)
    for peer in peers:
        pl.semaphore_signal(barrier, inc=1, device_id={"bin": peer}, device_id_type=MESH)
    pl.semaphore_wait(barrier, 2 + n_bin - 1)

    def halos(g):
        return [
            pltpu.make_async_remote_copy(
                src.at[g], dst.at[g], halo_sent.at[k, g], halo_got.at[k, g], device_id={"blk": side}, device_id_type=MESH
            )
            for k, (src, dst, side) in enumerate(((tails, from_left, right), (heads, from_right, left)))
        ]

    def table_copies():
        mine = table_ref.at[pl.ds(pl.multiple_of(bin_ * bins, bins), bins)]
        return [
            pltpu.make_async_remote_copy(
                own_table_ref, mine, table_sent.at[k], table_got.at[k], device_id={"bin": peer}, device_id_type=MESH
            )
            for k, peer in enumerate(peers)
        ]

    def pick_copies(g):
        return [
            pltpu.make_async_remote_copy(
                picks.at[g, pl.ds(peer * share, share)], got.at[bin_, g], pick_sent.at[k, g], pick_got.at[k, g],
                device_id={"bin": peer}, device_id_type=MESH,
            )
            for k, peer in enumerate(peers)
        ]

    def back_copies(g):
        return [
            pltpu.make_async_remote_copy(
                tends.at[peer, g], back_out.at[g, pl.ds(bin_ * share, share)], back_sent.at[k, g], back_got.at[k, g],
                device_id={"bin": peer}, device_id_type=MESH,
            )
            for k, peer in enumerate(peers)
        ]

    def own_back(g):
        return pltpu.make_async_copy(tends.at[bin_, g], back_out.at[g, pl.ds(bin_ * share, share)], own_sem.at[g])

    def out_copy(g):
        return pltpu.make_async_copy(settled_ref.at[g], settled_out.at[g], out_sem.at[g])

    def pack(g):
        to_left, to_right = left_order_ref[g] * nz * bx, right_order_ref[g] * nz * bx

        def level(z, carry):
            for x in range(3):
                rows = flat[pl.ds(to_left + z * bx + x, bins, stride=slots * nz * bx), :]
                heads[g, z, x] = rows.astype(bf16)
                rows = flat[pl.ds(to_right + z * bx + bx - 3 + x, bins, stride=slots * nz * bx), :]
                tails[g, z, x] = rows.astype(bf16)
            return carry

        lax.fori_loop(0, nz, level, 0)

    def pack_and_send(g, carry):
        pack(g)
        for copy in halos(g):
            copy.start()
        return carry

    lax.fori_loop(0, half, pack_and_send, 0)
    for copy in table_copies():
        copy.start()
    table_ref[pl.ds(pl.multiple_of(bin_ * bins, bins), bins), :] = own_table_ref[...]

    def pack_later(g, carry):
        pack(g)
        return carry

    lax.fori_loop(half, slots, pack_later, 0)

    def transport(g):
        row = order_ref[g]
        for first in range(0, bins, 8):
            fall = fall_ref[first : first + 8, :]
            start = (first * slots + row) * nz * bx

            def level(step, above, first=first, fall=fall, start=start):
                z = nz - 1 - step
                speed = jnp.broadcast_to(wind_ref[row, pl.ds(z, 1), :], (8, by))
                pos = speed > 0
                cw = courant * jnp.abs(speed)
                own = [flat[pl.ds(start + z * bx + x, 8, stride=slots * nz * bx), :] for x in range(bx)]
                head = [from_left[g, z, x, first : first + 8, :].astype(f32) for x in range(3)]
                tail = [from_right[g, z, x, first : first + 8, :].astype(f32) for x in range(3)]
                adv = advect_cells(head + own + tail, pos, cw * 0.5, cw * (1.0 / 6.0))
                for x in range(bx):
                    settled_ref[g, z, x, first : first + 8, :] = adv[x] - fall * (adv[x] - above[x])
                return tuple(adv)

            lax.fori_loop(0, nz, level, tuple(jnp.zeros((8, by), f32) for _ in range(bx)))

    def pick(g):
        def level(z, carry):
            for x in range(bx):
                picks[g, z, x] = settled_ref[g, z, x].astype(bf16)
            return carry

        lax.fori_loop(0, nz, level, 0)

    def collect(g):
        def pair(step, carry):
            zz, first = step // (bx // 2), step % (bx // 2) * 2
            for part in range(2):
                lanes = slice(part * by, (part + 1) * by)
                cells = [got[q, g, zz, first + part] for q in range(n_bin)]
                for q in range(n_bin):
                    cells_ref[q * bins : q * bins + bins, :] = cells[q].astype(f32)
                row = 0
                for i in range(n_bin * bins):
                    one = jnp.broadcast_to(cells_ref[i : i + 1, :], (bins, by)).astype(bf16)
                    for q in range(i // bins, n_bin):
                        prod_ref[row : row + bins, lanes] = one * cells[q]
                        row += bins
            total = jnp.dot(table_ref[...], prod_ref[...], preferred_element_type=f32).astype(bf16)
            for part in range(2):
                for q in range(n_bin):
                    tends[q, g, zz, first + part] = total[q * bins : q * bins + bins, part * by : (part + 1) * by]
            return carry

        lax.fori_loop(0, share * bx // 2, pair, 0)

    def slot(g, carry):
        for copy in halos(g):
            copy.wait_recv()

        @pl.when(blk == 0)
        def _():
            from_left[g] = jnp.zeros(from_left.shape[1:], bf16)

        @pl.when(blk == last)
        def _():
            from_right[g] = jnp.zeros(from_right.shape[1:], bf16)

        transport(g)
        out_copy(g).start()

        @pl.when(g < half)
        def _():
            pick(g)
            for copy in pick_copies(g):
                copy.start()
            got[bin_, g] = picks[g, pl.ds(bin_ * share, share)]
            for copy in halos(g + half):
                copy.start()

        @pl.when(g == 1)
        def _():
            for copy in table_copies():
                copy.wait_recv()

        @pl.when(jnp.logical_and(g >= 1, g <= half))
        def _():
            for copy in pick_copies(g - 1):
                copy.wait_recv()
            collect(g - 1)
            for copy in back_copies(g - 1):
                copy.start()
            own_back(g - 1).start()

        return carry

    lax.fori_loop(0, slots, slot, 0)

    for copy in table_copies():
        copy.wait_send()

    def finish(g, carry):
        for copy in halos(g):
            copy.wait_send()
        out_copy(g).wait()
        return carry

    lax.fori_loop(0, slots, finish, 0)

    def finish_active(g, carry):
        for copy in pick_copies(g):
            copy.wait_send()
        for copy in back_copies(g):
            copy.wait()
        own_back(g).wait()
        return carry

    lax.fori_loop(0, half, finish_active, 0)


def update_body(order_ref, count_ref, settled_ref, tend_ref, out_ref):
    bins, _, nz, bx, by = out_ref.shape
    flat_out = pieces(out_ref)
    on = jnp.full((bins, by), pl.program_id(0), jnp.int32) < count_ref[0]

    def level(z, carry):
        for x in range(bx):
            add = tend_ref[0, z, x].astype(f32) * time_step
            flat_out[pl.ds(z * bx + x, bins, stride=nz * bx), :] = settled_ref[0, z, x] + jnp.where(on, add, 0.0)
        return carry

    lax.fori_loop(0, nz, level, 0)


def pair_table(collection):
    t = jnp.transpose(collection, (2, 1, 0)).astype(f32)
    both = (t + jnp.transpose(t, (0, 2, 1))).astype(bf16)
    t = t.astype(bf16)
    parts = []
    for q in range(4):
        lo, hi = q * 16, q * 16 + 16
        rows = jnp.concatenate([t[:, lo:hi, lo:hi], both[:, lo:hi, hi:]], axis=2)
        parts.append(rows.reshape(t.shape[0], -1))
    return jnp.concatenate(parts, axis=1)


def local(spectrum, wind, fall_speed, collection, act_order, act_count):
    bins, slots, nz, bx, by = spectrum.shape
    n_blk, n_bin = lax.axis_size("blk"), lax.axis_size("bin")
    half, share, every = slots // 2, nz // n_bin, bins * n_bin
    order = act_order[0]
    left_order = lax.ppermute(order, "blk", [(i, (i + 1) % n_blk) for i in range(n_blk)])
    right_order = lax.ppermute(order, "blk", [((i + 1) % n_blk, i) for i in range(n_blk)])
    table = pair_table(collection)
    fall = jnp.broadcast_to((courant * fall_speed)[:, None], (bins, by))

    smem, vmem, hbm = (pl.BlockSpec(memory_space=s) for s in (pltpu.SMEM, pltpu.VMEM, pl.ANY))
    side = pltpu.VMEM((slots, nz, 3, bins, by), bf16)
    dma = pltpu.SemaphoreType.DMA
    settled, back = pl.pallas_call(
        step_body,
        in_specs=[smem] * 3 + [vmem] * 4,
        out_specs=[hbm] * 2,
        out_shape=[
            jax.ShapeDtypeStruct((slots, nz, bx, bins, by), f32),
            jax.ShapeDtypeStruct((half, nz, bx, bins, by), bf16),
        ],
        scratch_shapes=[
            pltpu.VMEM((every, table.shape[1]), bf16),
            side, side, side, side,
            pltpu.VMEM((slots, nz, bx, bins, by), f32),
            pltpu.VMEM((half, nz, bx, bins, by), bf16),
            pltpu.VMEM((n_bin, half, share, bx, bins, by), bf16),
            pltpu.VMEM((n_bin, half, share, bx, bins, by), bf16),
            pltpu.VMEM((every, by), f32),
            pltpu.VMEM((table.shape[1], 2 * by), bf16),
            dma((2, slots)), dma((2, slots)),
            dma((n_bin - 1, half)), dma((n_bin - 1, half)),
            dma((n_bin - 1, half)), dma((n_bin - 1, half)),
            dma((n_bin - 1,)), dma((n_bin - 1,)),
            dma((slots,)), dma((half,)),
        ],
        compiler_params=pltpu.CompilerParams(collective_id=0, has_side_effects=True, vmem_limit_bytes=48 << 20),
    )(order, left_order, right_order, spectrum, wind, fall, table)

    return pl.pallas_call(
        update_body,
        grid_spec=pltpu.PrefetchScalarGridSpec(
            num_scalar_prefetch=2,
            grid=(slots,),
            in_specs=[
                pl.BlockSpec((1, nz, bx, bins, by), lambda g, o, c: (g, 0, 0, 0, 0)),
                pl.BlockSpec((1, nz, bx, bins, by), lambda g, o, c: (jnp.minimum(g, half - 1), 0, 0, 0, 0)),
            ],
            out_specs=pl.BlockSpec((bins, 1, nz, bx, by), lambda g, o, c: (0, o[g], 0, 0, 0)),
        ),
        out_shape=jax.ShapeDtypeStruct(spectrum.shape, f32),
    )(order, act_count, settled, back)


def solution(mesh):
    return jax.shard_map(
        local,
        mesh=mesh,
        in_specs=(
            P("bin", None, None, "blk", None),
            P(),
            P("bin"),
            P(None, None, "bin"),
            P("blk", None),
            P("blk"),
        ),
        out_specs=P("bin", None, None, "blk", None),
        check_vma=False,
    )
```

time: 182 us -> 127 us (0.70)
  the two profiles are of different devices: /device:TPU:1 before, /device:TPU:5 now
where the time goes in v2:
time: 127 us; the launch traced here: 126 us
  Pallas kernels  113 us (89%)
  local copies, waits for them, and re-layouts  4.93 us (4%)
  starting transfers between devices  3.87 us (3%)
  waiting for transfers between devices  2.16 us (2%)
  other arithmetic  1.97 us (2%)
    pallas_call x1, Pallas kernels, local(): pl.pallas_call(step_body, in_specs=[smem] * 3 + [vmem] * 4, out_specs=[hb...  102 us
    pallas_call x1, Pallas kernels, local(): pl.pallas_call(update_body, grid_spec=pltpu.PrefetchScalarGridSpec(num_sc...  10.9 us
    unnamed x6, local copies, waits for them, and re-layouts  3.93 us
    ppermute x1, starting transfers between devices, local(): lax.ppermute(order, 'blk', [(i, (i + 1) % n_blk) for i in range(n_blk)])  3.87 us
  transfers between devices with their start and end apart: 2, of which 1 were waited for; matrix products, arithmetic and copies ran while one was open for 4% of the time, Pallas kernels for 0%

profile of v2, /device:TPU:5, one launch (start us, length us, event | category | flops | bytes accessed | tf_op | source)
XLA Modules:
  0.0 126.2 jit_solution(1511085670135807979)
XLA Ops:
  0.0 0.0 collective-permute-start.1
  0.0 3.9 %collective-permute-start = (s32[8]{0:T(128)}, s32[8]{0:T(128)S(1)}, u32[]{:S(2)}, u32[]{:S(2)}) collective-permute-start(s32[8]{0:T(128)} %bitcast.8), channel_id=1, source_target_pairs={{0,4},{4,8},{8,12},{12,16},{16,20},{20,24},{24,28},{28,32},{32,36}... | collective-permute-start | bytes 104 | tf_op jit(solution)/shard_map/ppermute | solution.py:292
  3.9 1.3 %copy.7 = bf16[64,64,16]{0,2,1:T(8,128)(2,1)S(1)} copy(bf16[64,64,16]{1,2,0:T(8,128)(2,1)} %param.9) | data formatting | bytes 262144 | tf_op args[3]
  5.2 1.0 fusion
  6.2 0.1 slice.33
  6.3 0.1 slice.31
  6.4 0.1 slice.29
  7.2 0.7 broadcast_multiply_fusion
  7.8 0.8 copy.12.wind_ref
  8.6 0.1 fusion.1
  8.8 0.1 pad_maximum_fusion.2
  8.9 0.1 reshape.14
  9.0 0.1 pad_maximum_fusion.1
  9.1 0.1 reshape.13
  9.2 0.1 pad_maximum_fusion.3
  9.4 0.1 reshape.15
  9.5 0.1 reshape.16
  9.6 0.0 collective-permute-done.1.right_order_ref
  9.7 2.2 %collective-permute-done.left_order_ref = s32[8]{0:T(128)S(1)} collective-permute-done((s32[8]{0:T(128)}, s32[8]{0:T(128)S(1)}, u32[]{:S(2)}, u32[]{:S(2)}) %collective-permute-start) | collective-permute-done | bytes 64 | tf_op jit(solution)/shard_map/ppermute | solution.py:292
  11.8 0.1 broadcast_in_dim.2.fall_ref
  11.9 0.0 copy-start.1
  11.9 0.7 copy-done.1
  12.5 101.6 %shard_map.64 = (f32[8,12,8,16,128]{4,3,2,1,0:T(8,128)}, bf16[4,12,8,16,128]{4,3,2,1,0:T(8,128)(2,1)S(1)}) custom-call(s32[8]{0:T(128)S(1)} %bitcast.10, s32[8]{0:T(128)S(1)} %collective-permute-done.left_order_ref, s32[8]{0:T(128)S(1)} %collective-permute-done.1.right_order_ref, f32[16,8,12,8,128]{4,3,2,1,0:T(8,128)} %spec_ref.1, ...), custom_call_target="tpu_custom_call" | custom-call | tf_op jit(solution)/shard_map/pallas_call | solution.py:300
  114.2 0.0 copy-start
  114.2 1.1 copy-done
  115.3 10.9 %shard_map.65 = f32[16,8,12,8,128]{4,3,2,1,0:T(8,128)} custom-call(s32[8]{0:T(128)} %bitcast.9, s32[1]{0:T(128)S(6)} %copy.13.count_ref, f32[8,12,8,16,128]{4,3,2,1,0:T(8,128)} %get-tuple-element.7.settled_ref, bf16[4,12,8,16,128]{4,3,2,1,0:T(8,128)(2,1)} %copy-done), custom_call_target="tpu_custom_call" | custom-call | tf_op jit(solution)/shard_map/pallas_call | solution.py:326
  (5 shorter events, 0.1 us)
Async XLA Ops:
  0.0 9.6 %collective-permute-start.1 = (s32[8]{0:T(128)}, s32[8]{0:T(128)S(1)}, u32[]{:S(2)}, u32[]{:S(2)}) collective-permute-start(s32[8]{0:T(128)} %bitcast.7), channel_id=1, source_target_pairs={{4,0},{8,4},{12,8},{16,12},{20,16},{24,20},{28,24},{32,28},{36,32}... | collective-permute-start | bytes 104 | tf_op jit(solution)/shard_map/ppermute | solution.py:293
  0.0 11.8 %collective-permute-start = (s32[8]{0:T(128)}, s32[8]{0:T(128)S(1)}, u32[]{:S(2)}, u32[]{:S(2)}) collective-permute-start(s32[8]{0:T(128)} %bitcast.8), channel_id=1, source_target_pairs={{0,4},{4,8},{8,12},{12,16},{16,20},{20,24},{24,28},{28,32},{32,36}... | collective-permute-start | bytes 104 | tf_op jit(solution)/shard_map/ppermute | solution.py:292
  11.9 0.7 copy-start.1
  114.2 1.2 copy-start

commit v3 on v2

--- a/solution.py
+++ b/solution.py
@@ -50,27 +50,46 @@
 
 
 def step_body(
-    order_ref, left_order_ref, right_order_ref, spec_ref, wind_ref, fall_ref, own_table_ref,
-    settled_out, back_out,
-    table_ref, heads, tails, from_left, from_right, settled_ref, picks, got, tends, cells_ref, prod_ref,
-    halo_sent, halo_got, pick_sent, pick_got, back_sent, back_got, table_sent, table_got, out_sem, own_sem,
+    order_rows, fall_speed_ref, spec_hbm, wind_ref, own_table_ref,
+    settled_ref, back_out,
+    spec_ref, rows_got, orders, own_order, fall_ref,
+    table_ref, heads, tails, from_left, from_right, picks, got, tends, cells_ref, prod_ref,
+    thirds, third_left, third_on, third_right, third_sent, third_got, on_sent, on_got,
+    halo_sent, halo_got, pick_sent, pick_got, back_sent, back_got, table_sent, table_got, own_sem,
+    spec_sem, rows_sent, rows_recv, orders_sem, own_order_sem,
 ):
-    bins, slots, nz, bx, by = spec_ref.shape
+    bins, slots, nz, bx, by = spec_hbm.shape
     half = slots // 2
     flat = pieces(spec_ref)
+    spec_copies = [pltpu.make_async_copy(spec_hbm.at[b], spec_ref.at[b], spec_sem.at[b]) for b in range(bins)]
+    for copy in spec_copies:
+        copy.start()
     blk, bin_ = lax.axis_index("blk"), lax.axis_index("bin")
     n_blk, n_bin = lax.axis_size("blk"), lax.axis_size("bin")
     share = nz // n_bin
     last = n_blk - 1
     right, left = lax.rem(blk + 1, n_blk), lax.rem(blk + last, n_blk)
+    right2, left2 = lax.rem(blk + 2, n_blk), lax.rem(blk + last - 1, n_blk)
+    sibling, across = bin_ + 1 - 2 * lax.rem(bin_, 2), lax.rem(bin_ + 2, n_bin)
     peers = [lax.rem(bin_ + k, n_bin) for k in range(1, n_bin)]
 
     barrier = pltpu.get_barrier_semaphore()
-    for side in (left, right):
+    for side in (left, right, left2, right2):
         pl.semaphore_signal(barrier, inc=1, device_id={"blk": side}, device_id_type=MESH)
     for peer in peers:
         pl.semaphore_signal(barrier, inc=1, device_id={"bin": peer}, device_id_type=MESH)
-    pl.semaphore_wait(barrier, 2 + n_bin - 1)
+    pl.semaphore_wait(barrier, 4 + n_bin - 1)
+
+    row_copies = [
+        pltpu.make_async_remote_copy(
+            order_rows, rows_got.at[k], rows_sent.at[k], rows_recv.at[k], device_id={"blk": side}, device_id_type=MESH
+        )
+        for k, side in enumerate((right, left, right2))
+    ]
+    for copy in row_copies:
+        copy.start()
+    for b in range(bins):
+        fall_ref[b : b + 1, :] = jnp.full((1, by), fall_speed_ref[b], f32) * courant
 
     def halos(g):
         return [
@@ -80,14 +99,28 @@
             for k, (src, dst, side) in enumerate(((tails, from_left, right), (heads, from_right, left)))
         ]
 
-    def table_copies():
-        mine = table_ref.at[pl.ds(pl.multiple_of(bin_ * bins, bins), bins)]
-        return [
-            pltpu.make_async_remote_copy(
-                own_table_ref, mine, table_sent.at[k], table_got.at[k], device_id={"bin": peer}, device_id_type=MESH
-            )
-            for k, peer in enumerate(peers)
-        ]
+    def table_part(q):
+        return table_ref.at[pl.ds(pl.multiple_of(q * bins, bins), bins)]
+
+    def table_copy(k):
+        src, part, peer = (
+            (own_table_ref, table_part(bin_), sibling),
+            (own_table_ref, table_part(bin_), across),
+            (table_part(across), table_part(across), sibling),
+        )[k]
+        return pltpu.make_async_remote_copy(
+            src, part, table_sent.at[k], table_got.at[k], device_id={"bin": peer}, device_id_type=MESH
+        )
+
+    def third_copy(r):
+        return pltpu.make_async_remote_copy(
+            thirds.at[r], third_left.at[r], third_sent.at[r], third_got.at[r], device_id={"blk": right}, device_id_type=MESH
+        )
+
+    def on_copy(g):
+        return pltpu.make_async_remote_copy(
+            third_on.at[g], third_right.at[g], on_sent.at[g], on_got.at[g], device_id={"blk": left2}, device_id_type=MESH
+        )
 
     def pick_copies(g):
         return [
@@ -110,21 +143,37 @@
     def own_back(g):
         return pltpu.make_async_copy(tends.at[bin_, g], back_out.at[g, pl.ds(bin_ * share, share)], own_sem.at[g])
 
-    def out_copy(g):
-        return pltpu.make_async_copy(settled_ref.at[g], settled_out.at[g], out_sem.at[g])
-
     def pack(g):
-        to_left, to_right = left_order_ref[g] * nz * bx, right_order_ref[g] * nz * bx
+        to_left, to_right = orders[0, g, 0] * nz * bx, orders[1, g, 0] * nz * bx
 
         def level(z, carry):
-            for x in range(3):
+            for x in range(2):
                 rows = flat[pl.ds(to_left + z * bx + x, bins, stride=slots * nz * bx), :]
                 heads[g, z, x] = rows.astype(bf16)
-                rows = flat[pl.ds(to_right + z * bx + bx - 3 + x, bins, stride=slots * nz * bx), :]
+                rows = flat[pl.ds(to_right + z * bx + bx - 2 + x, bins, stride=slots * nz * bx), :]
                 tails[g, z, x] = rows.astype(bf16)
             return carry
 
         lax.fori_loop(0, nz, level, 0)
+
+    def pack_third(r, carry):
+        def level(z, inner):
+            low = flat[pl.ds(r * nz * bx + z * bx + 2, bins, stride=slots * nz * bx), :]
+            high = flat[pl.ds(r * nz * bx + z * bx + bx - 3, bins, stride=slots * nz * bx), :]
+            pos = jnp.broadcast_to(wind_ref[z, pl.ds(r, 1), :], (bins, by)) > 0
+            thirds[r, z] = jnp.where(pos, high, low).astype(bf16)
+            return inner
+
+        lax.fori_loop(0, nz, level, 0)
+        third_copy(r).start()
+        return carry
+
+    def pass_on(g, carry):
+        row = orders[2, g, 0]
+        for z in range(nz):
+            third_on[g, z] = third_left[row, z]
+        on_copy(g).start()
+        return carry
 
     def pack_and_send(g, carry):
         pack(g)
@@ -132,9 +181,20 @@
             copy.start()
         return carry
 
+    own_order_copy = pltpu.make_async_copy(order_rows, own_order, own_order_sem)
+    own_order_copy.start()
+    for copy in spec_copies:
+        copy.wait()
+    lax.fori_loop(0, slots, pack_third, 0)
+    for copy in row_copies:
+        copy.wait_recv()
+    orders_copy = pltpu.make_async_copy(rows_got, orders, orders_sem)
+    orders_copy.start()
+    orders_copy.wait()
+    own_order_copy.wait()
     lax.fori_loop(0, half, pack_and_send, 0)
-    for copy in table_copies():
-        copy.start()
+    table_copy(0).start()
+    table_copy(1).start()
     table_ref[pl.ds(pl.multiple_of(bin_ * bins, bins), bins), :] = own_table_ref[...]
 
     def pack_later(g, carry):
@@ -143,20 +203,33 @@
 
     lax.fori_loop(half, slots, pack_later, 0)
 
+    def third_arrived(r, carry):
+        third_copy(r).wait_recv()
+        return carry
+
+    lax.fori_loop(0, slots, third_arrived, 0)
+    lax.fori_loop(0, slots, pass_on, 0)
+
+    @pl.when(blk == 0)
+    def _():
+        third_left[...] = jnp.zeros(third_left.shape, bf16)
+
     def transport(g):
-        row = order_ref[g]
+        row = own_order[g, 0]
         for first in range(0, bins, 8):
             fall = fall_ref[first : first + 8, :]
             start = (first * slots + row) * nz * bx
 
             def level(step, above, first=first, fall=fall, start=start):
                 z = nz - 1 - step
-                speed = jnp.broadcast_to(wind_ref[row, pl.ds(z, 1), :], (8, by))
+                speed = jnp.broadcast_to(wind_ref[z, pl.ds(row, 1), :], (8, by))
                 pos = speed > 0
                 cw = courant * jnp.abs(speed)
                 own = [flat[pl.ds(start + z * bx + x, 8, stride=slots * nz * bx), :] for x in range(bx)]
-                head = [from_left[g, z, x, first : first + 8, :].astype(f32) for x in range(3)]
-                tail = [from_right[g, z, x, first : first + 8, :].astype(f32) for x in range(3)]
+                head = [from_left[g, z, x, first : first + 8, :].astype(f32) for x in range(2)]
+                tail = [from_right[g, z, x, first : first + 8, :].astype(f32) for x in range(2)]
+                head = [third_left[row, z, first : first + 8, :].astype(f32)] + head
+                tail = tail + [third_right[g, z, first : first + 8, :].astype(f32)]
                 adv = advect_cells(head + own + tail, pos, cw * 0.5, cw * (1.0 / 6.0))
                 for x in range(bx):
                     settled_ref[g, z, x, first : first + 8, :] = adv[x] - fall * (adv[x] - above[x])
@@ -195,6 +268,7 @@
         lax.fori_loop(0, share * bx // 2, pair, 0)
 
     def slot(g, carry):
+        on_copy(g).wait_recv()
         for copy in halos(g):
             copy.wait_recv()
 
@@ -205,9 +279,9 @@
         @pl.when(blk == last)
         def _():
             from_right[g] = jnp.zeros(from_right.shape[1:], bf16)
+            third_right[g] = jnp.zeros(third_right.shape[1:], bf16)
 
         transport(g)
-        out_copy(g).start()
 
         @pl.when(g < half)
         def _():
@@ -218,10 +292,15 @@
             for copy in halos(g + half):
                 copy.start()
 
+        @pl.when(g == 0)
+        def _():
+            table_copy(1).wait_recv()
+            table_copy(2).start()
+
         @pl.when(g == 1)
         def _():
-            for copy in table_copies():
-                copy.wait_recv()
+            table_copy(0).wait_recv()
+            table_copy(2).wait_recv()
 
         @pl.when(jnp.logical_and(g >= 1, g <= half))
         def _():
@@ -236,13 +315,14 @@
 
     lax.fori_loop(0, slots, slot, 0)
 
-    for copy in table_copies():
+    for copy in row_copies + [table_copy(k) for k in range(3)]:
         copy.wait_send()
 
     def finish(g, carry):
+        third_copy(g).wait_send()
+        on_copy(g).wait_send()
         for copy in halos(g):
             copy.wait_send()
-        out_copy(g).wait()
         return carry
 
     lax.fori_loop(0, slots, finish, 0)
@@ -258,18 +338,42 @@
     lax.fori_loop(0, half, finish_active, 0)
 
 
-def update_body(order_ref, count_ref, settled_ref, tend_ref, out_ref):
-    bins, _, nz, bx, by = out_ref.shape
-    flat_out = pieces(out_ref)
-    on = jnp.full((bins, by), pl.program_id(0), jnp.int32) < count_ref[0]
-
-    def level(z, carry):
-        for x in range(bx):
-            add = tend_ref[0, z, x].astype(f32) * time_step
-            flat_out[pl.ds(z * bx + x, bins, stride=nz * bx), :] = settled_ref[0, z, x] + jnp.where(on, add, 0.0)
-        return carry
-
-    lax.fori_loop(0, nz, level, 0)
+def update_body(order_ref, count_ref, settled_ref, tend_ref, out_ref, rows_ref, out_sem):
+    bins, slots, nz, bx, by = out_ref.shape
+    half = slots // 2
+
+    def copy(g):
+        return pltpu.make_async_copy(rows_ref.at[g], out_ref.at[:, order_ref[g]], out_sem.at[g])
+
+    def active(g, carry):
+        on = jnp.full((bx, bins, by), g, jnp.int32) < count_ref[0]
+
+        def level(z, inner):
+            add = tend_ref[g, z].astype(f32) * time_step
+            rows_ref[g, :, z] = jnp.swapaxes(settled_ref[g, z] + jnp.where(on, add, 0.0), 0, 1)
+            return inner
+
+        lax.fori_loop(0, nz, level, 0)
+        copy(g).start()
+        return carry
+
+    def idle(g, carry):
+        def level(z, inner):
+            rows_ref[g, :, z] = jnp.swapaxes(settled_ref[g, z], 0, 1)
+            return inner
+
+        lax.fori_loop(0, nz, level, 0)
+        copy(g).start()
+        return carry
+
+    lax.fori_loop(0, half, active, 0)
+    lax.fori_loop(half, slots, idle, 0)
+
+    def finish(g, carry):
+        copy(g).wait()
+        return carry
+
+    lax.fori_loop(0, slots, finish, 0)
 
 
 def pair_table(collection):
@@ -289,52 +393,52 @@
     n_blk, n_bin = lax.axis_size("blk"), lax.axis_size("bin")
     half, share, every = slots // 2, nz // n_bin, bins * n_bin
     order = act_order[0]
-    left_order = lax.ppermute(order, "blk", [(i, (i + 1) % n_blk) for i in range(n_blk)])
-    right_order = lax.ppermute(order, "blk", [((i + 1) % n_blk, i) for i in range(n_blk)])
+    order_rows = jnp.broadcast_to(order[:, None], (slots, by))
     table = pair_table(collection)
-    fall = jnp.broadcast_to((courant * fall_speed)[:, None], (bins, by))
 
     smem, vmem, hbm = (pl.BlockSpec(memory_space=s) for s in (pltpu.SMEM, pltpu.VMEM, pl.ANY))
-    side = pltpu.VMEM((slots, nz, 3, bins, by), bf16)
+    side = pltpu.VMEM((slots, nz, 2, bins, by), bf16)
+    third = pltpu.VMEM((slots, nz, bins, by), bf16)
     dma = pltpu.SemaphoreType.DMA
     settled, back = pl.pallas_call(
         step_body,
-        in_specs=[smem] * 3 + [vmem] * 4,
-        out_specs=[hbm] * 2,
+        in_specs=[vmem, smem, pl.BlockSpec(memory_space=pltpu.HBM), vmem, vmem],
+        out_specs=[vmem, hbm],
         out_shape=[
             jax.ShapeDtypeStruct((slots, nz, bx, bins, by), f32),
             jax.ShapeDtypeStruct((half, nz, bx, bins, by), bf16),
         ],
         scratch_shapes=[
+            pltpu.VMEM(spectrum.shape, f32),
+            pltpu.VMEM((3, slots, by), jnp.int32),
+            pltpu.SMEM((3, slots, by), jnp.int32),
+            pltpu.SMEM((slots, by), jnp.int32),
+            pltpu.VMEM((bins, by), f32),
             pltpu.VMEM((every, table.shape[1]), bf16),
             side, side, side, side,
-            pltpu.VMEM((slots, nz, bx, bins, by), f32),
             pltpu.VMEM((half, nz, bx, bins, by), bf16),
             pltpu.VMEM((n_bin, half, share, bx, bins, by), bf16),
             pltpu.VMEM((n_bin, half, share, bx, bins, by), bf16),
             pltpu.VMEM((every, by), f32),
             pltpu.VMEM((table.shape[1], 2 * by), bf16),
+            third, third, third, third,
+            dma((slots,)), dma((slots,)), dma((slots,)), dma((slots,)),
             dma((2, slots)), dma((2, slots)),
             dma((n_bin - 1, half)), dma((n_bin - 1, half)),
             dma((n_bin - 1, half)), dma((n_bin - 1, half)),
             dma((n_bin - 1,)), dma((n_bin - 1,)),
-            dma((slots,)), dma((half,)),
+            dma((half,)), dma((bins,)), dma((3,)), dma((3,)), dma(()), dma(()),
         ],
-        compiler_params=pltpu.CompilerParams(collective_id=0, has_side_effects=True, vmem_limit_bytes=48 << 20),
-    )(order, left_order, right_order, spectrum, wind, fall, table)
+        compiler_params=pltpu.CompilerParams(collective_id=0, has_side_effects=True, vmem_limit_bytes=42 << 20),
+    )(order_rows, fall_speed, spectrum, jnp.transpose(wind, (1, 0, 2)), table)
 
     return pl.pallas_call(
         update_body,
-        grid_spec=pltpu.PrefetchScalarGridSpec(
-            num_scalar_prefetch=2,
-            grid=(slots,),
-            in_specs=[
-                pl.BlockSpec((1, nz, bx, bins, by), lambda g, o, c: (g, 0, 0, 0, 0)),
-                pl.BlockSpec((1, nz, bx, bins, by), lambda g, o, c: (jnp.minimum(g, half - 1), 0, 0, 0, 0)),
-            ],
-            out_specs=pl.BlockSpec((bins, 1, nz, bx, by), lambda g, o, c: (0, o[g], 0, 0, 0)),
-        ),
+        in_specs=[smem, smem, vmem, vmem],
+        out_specs=hbm,
         out_shape=jax.ShapeDtypeStruct(spectrum.shape, f32),
+        scratch_shapes=[pltpu.VMEM((slots, bins, nz, bx, by), f32), dma((slots,))],
+        compiler_params=pltpu.CompilerParams(vmem_limit_bytes=16 << 20),
     )(order, act_count, settled, back)
 
 

time: 127 us -> 105 us (0.83)
  the two profiles are of different devices: /device:TPU:5 before, /device:TPU:1 now
where the time goes in v3:
time: 105 us
  Pallas kernels  98.7 us (94%)
  local copies, waits for them, and re-layouts  4.43 us (4%)
  other arithmetic  1.31 us (1%)
    pallas_call x1, Pallas kernels, local(): pl.pallas_call(step_body, in_specs=[vmem, smem, pl.BlockSpec(memory_space...  94.9 us
    pallas_call x1, Pallas kernels, local(): pl.pallas_call(update_body, in_specs=[smem, smem, vmem, vmem], out_specs=...  3.74 us
    unnamed x7, local copies, waits for them, and re-layouts  2.77 us

profile of v3, /device:TPU:1, one launch (start us, length us, event | category | flops | bytes accessed | tf_op | source)
XLA Modules:
  0.0 105.2 jit_solution(8130464352666303445)
XLA Ops:
  0.0 0.0 copy-start.1
  0.7 0.7 broadcast_in_dim.2.order_rows
  1.4 1.3 %copy.7 = bf16[64,64,16]{0,2,1:T(8,128)(2,1)S(1)} copy(bf16[64,64,16]{1,2,0:T(8,128)(2,1)} %param.9) | data formatting | bytes 262144 | tf_op args[3]
  2.7 1.0 fusion
  3.8 0.1 slice.33
  3.8 0.1 slice.31
  3.9 0.1 slice.29
  4.0 0.1 fusion.1
  4.2 0.1 pad_maximum_fusion.2
  4.3 0.1 reshape.14
  4.4 0.1 pad_maximum_fusion.1
  4.5 0.1 reshape.13
  4.6 0.1 pad_maximum_fusion.3
  4.8 0.1 reshape.15
  4.9 0.1 reshape.16
  5.0 0.0 copy-start
  5.1 0.8 copy-done
  5.8 0.0 copy-start.2
  5.9 0.7 copy-done.2
  6.5 94.9 %shard_map.64 = (f32[8,12,8,16,128]{4,3,2,1,0:T(8,128)S(1)}, bf16[4,12,8,16,128]{4,3,2,1,0:T(8,128)(2,1)S(1)}) custom-call(s32[8,128]{1,0:T(8,128)S(1)} %broadcast_in_dim.2.order_rows, f32[16]{0:T(128)S(1)} %copy-done.2, f32[16,8,12,8,128]{4,3,2,1,0:T(8,128)} %spec_hbm.1, f32[12,8,128]{2,1,0:T(8,128)S(1)} %bitcast.8, ...), custom_call_target="tpu_custom_call" | custom-call | tf_op jit(solution)/shard_map/pallas_call | solution.py:403
  101.4 0.0 copy-done.1
  101.4 3.7 %shard_map.65 = f32[16,8,12,8,128]{4,3,2,1,0:T(8,128)} custom-call(s32[8]{0:T(128)S(1)} %bitcast.10, s32[1]{0:T(128)S(6)} %copy.12.count_ref, f32[8,12,8,16,128]{4,3,2,1,0:T(8,128)S(1)} %get-tuple-element.7.settled_ref, bf16[4,12,8,16,128]{4,3,2,1,0:T(8,128)(2,1)S(1)} %get-tuple-element.8.tend_ref), custom_call_target="tpu_custom_call" | custom-call | tf_op jit(solution)/shard_map/pallas_call | solution.py:435
  (5 shorter events, 0.1 us)
Async XLA Ops:
  0.0 101.4 %copy-start.1 = (s32[1,8]{1,0:T(1,128)S(1)}, s32[1,8]{1,0:T(1,128)}, u32[]{:S(2)}) copy-start(s32[1,8]{1,0:T(1,128)} %param.10) | copy-start | bytes 100
  5.0 0.8 copy-start
  5.8 0.7 copy-start.2

commit v4 on v3

--- a/solution.py
+++ b/solution.py
@@ -49,21 +49,57 @@
     return [jnp.where(pos, moved[i], moved[7 - i]) for i in range(8)]
 
 
+def pair_table(coll_ref, by_bin, sums, table_ref):
+    every, bins, _ = coll_ref.shape
+    by_bin[...] = jnp.swapaxes(coll_ref[...].astype(f32), 0, 1)
+
+    def one_bin(k, carry):
+        both = by_bin[k]
+        by_bin[k] = both + both.T
+        return carry
+
+    lax.fori_loop(0, bins, one_bin, 0)
+    sums[...] = jnp.swapaxes(by_bin[...], 0, 1)
+    lane = lax.broadcasted_iota(jnp.int32, (bins, every), 1)
+    column = 0
+    for first in range(0, every, bins):
+        own_group = lane < first + bins
+        parts = []
+        for i in range(first, first + bins):
+            parts.append(jnp.where(own_group, coll_ref[i].astype(f32), sums[i])[:, first:])
+        block = jnp.concatenate(parts, axis=1).astype(bf16)
+        table_ref[:, column : column + block.shape[1]] = block
+        column += block.shape[1]
+
+
 def step_body(
-    order_rows, fall_speed_ref, spec_hbm, wind_ref, own_table_ref,
+    order_hbm, fall_hbm, spec_hbm, wind_hbm, coll_hbm,
     settled_ref, back_out,
-    spec_ref, rows_got, orders, own_order, fall_ref,
+    spec_ref, wind_ref, coll_ref, own_table_ref, by_bin, sums, order_rows, fall_speed_ref,
+    rows_got, orders, own_order, fall_ref,
     table_ref, heads, tails, from_left, from_right, picks, got, tends, cells_ref, prod_ref,
     thirds, third_left, third_on, third_right, third_sent, third_got, on_sent, on_got,
     halo_sent, halo_got, pick_sent, pick_got, back_sent, back_got, table_sent, table_got, own_sem,
-    spec_sem, rows_sent, rows_recv, orders_sem, own_order_sem,
+    spec_sem, small_sem, rows_sent, rows_recv, orders_sem,
 ):
     bins, slots, nz, bx, by = spec_hbm.shape
     half = slots // 2
     flat = pieces(spec_ref)
-    spec_copies = [pltpu.make_async_copy(spec_hbm.at[b], spec_ref.at[b], spec_sem.at[b]) for b in range(bins)]
-    for copy in spec_copies:
+    small_copies = [
+        pltpu.make_async_copy(src, dst, small_sem.at[k])
+        for k, (src, dst) in enumerate(
+            ((order_hbm, order_rows), (order_hbm, own_order), (fall_hbm, fall_speed_ref), (wind_hbm, wind_ref), (coll_hbm, coll_ref))
+        )
+    ]
+    for copy in small_copies[:4]:
         copy.start()
+
+    def spec_copy(r):
+        return pltpu.make_async_copy(spec_hbm.at[:, r], spec_ref.at[:, r], spec_sem.at[r])
+
+    for r in range(slots):
+        spec_copy(r).start()
+    small_copies[4].start()
     blk, bin_ = lax.axis_index("blk"), lax.axis_index("bin")
     n_blk, n_bin = lax.axis_size("blk"), lax.axis_size("bin")
     share = nz // n_bin
@@ -86,10 +122,11 @@
         )
         for k, side in enumerate((right, left, right2))
     ]
+    small_copies[0].wait()
     for copy in row_copies:
         copy.start()
-    for b in range(bins):
-        fall_ref[b : b + 1, :] = jnp.full((1, by), fall_speed_ref[b], f32) * courant
+    for copy in small_copies[1:4]:
+        copy.wait()
 
     def halos(g):
         return [
@@ -144,7 +181,7 @@
         return pltpu.make_async_copy(tends.at[bin_, g], back_out.at[g, pl.ds(bin_ * share, share)], own_sem.at[g])
 
     def pack(g):
-        to_left, to_right = orders[0, g, 0] * nz * bx, orders[1, g, 0] * nz * bx
+        to_left, to_right = orders[0, 0, g] * nz * bx, orders[1, 0, g] * nz * bx
 
         def level(z, carry):
             for x in range(2):
@@ -157,6 +194,8 @@
         lax.fori_loop(0, nz, level, 0)
 
     def pack_third(r, carry):
+        spec_copy(r).wait()
+
         def level(z, inner):
             low = flat[pl.ds(r * nz * bx + z * bx + 2, bins, stride=slots * nz * bx), :]
             high = flat[pl.ds(r * nz * bx + z * bx + bx - 3, bins, stride=slots * nz * bx), :]
@@ -169,7 +208,7 @@
         return carry
 
     def pass_on(g, carry):
-        row = orders[2, g, 0]
+        row = orders[2, 0, g]
         for z in range(nz):
             third_on[g, z] = third_left[row, z]
         on_copy(g).start()
@@ -181,18 +220,17 @@
             copy.start()
         return carry
 
-    own_order_copy = pltpu.make_async_copy(order_rows, own_order, own_order_sem)
-    own_order_copy.start()
-    for copy in spec_copies:
-        copy.wait()
     lax.fori_loop(0, slots, pack_third, 0)
     for copy in row_copies:
         copy.wait_recv()
     orders_copy = pltpu.make_async_copy(rows_got, orders, orders_sem)
     orders_copy.start()
     orders_copy.wait()
-    own_order_copy.wait()
     lax.fori_loop(0, half, pack_and_send, 0)
+    for b in range(bins):
+        fall_ref[b : b + 1, :] = jnp.full((1, by), fall_speed_ref[b], f32) * courant
+    small_copies[4].wait()
+    pair_table(coll_ref, by_bin, sums, own_table_ref)
     table_copy(0).start()
     table_copy(1).start()
     table_ref[pl.ds(pl.multiple_of(bin_ * bins, bins), bins), :] = own_table_ref[...]
@@ -215,7 +253,7 @@
         third_left[...] = jnp.zeros(third_left.shape, bf16)
 
     def transport(g):
-        row = own_order[g, 0]
+        row = own_order[0, g]
         for first in range(0, bins, 8):
             fall = fall_ref[first : first + 8, :]
             start = (first * slots + row) * nz * bx
@@ -376,25 +414,14 @@
     lax.fori_loop(0, slots, finish, 0)
 
 
-def pair_table(collection):
-    t = jnp.transpose(collection, (2, 1, 0)).astype(f32)
-    both = (t + jnp.transpose(t, (0, 2, 1))).astype(bf16)
-    t = t.astype(bf16)
-    parts = []
-    for q in range(4):
-        lo, hi = q * 16, q * 16 + 16
-        rows = jnp.concatenate([t[:, lo:hi, lo:hi], both[:, lo:hi, hi:]], axis=2)
-        parts.append(rows.reshape(t.shape[0], -1))
-    return jnp.concatenate(parts, axis=1)
-
-
 def local(spectrum, wind, fall_speed, collection, act_order, act_count):
     bins, slots, nz, bx, by = spectrum.shape
     n_blk, n_bin = lax.axis_size("blk"), lax.axis_size("bin")
     half, share, every = slots // 2, nz // n_bin, bins * n_bin
     order = act_order[0]
-    order_rows = jnp.broadcast_to(order[:, None], (slots, by))
-    table = pair_table(collection)
+    pairs = sum(bins * (every - first) for first in range(0, every, bins))
+
+    inputs = (act_order, fall_speed, spectrum, jnp.transpose(wind, (1, 0, 2)), jnp.transpose(collection, (0, 2, 1)))
 
     smem, vmem, hbm = (pl.BlockSpec(memory_space=s) for s in (pltpu.SMEM, pltpu.VMEM, pl.ANY))
     side = pltpu.VMEM((slots, nz, 2, bins, by), bf16)
@@ -402,7 +429,7 @@
     dma = pltpu.SemaphoreType.DMA
     settled, back = pl.pallas_call(
         step_body,
-        in_specs=[vmem, smem, pl.BlockSpec(memory_space=pltpu.HBM), vmem, vmem],
+        in_specs=[pl.BlockSpec(memory_space=pltpu.HBM)] * 5,
         out_specs=[vmem, hbm],
         out_shape=[
             jax.ShapeDtypeStruct((slots, nz, bx, bins, by), f32),
@@ -410,27 +437,34 @@
         ],
         scratch_shapes=[
             pltpu.VMEM(spectrum.shape, f32),
-            pltpu.VMEM((3, slots, by), jnp.int32),
-            pltpu.SMEM((3, slots, by), jnp.int32),
-            pltpu.SMEM((slots, by), jnp.int32),
+            pltpu.VMEM((nz, slots, by), f32),
+            pltpu.VMEM((every, bins, every), bf16),
+            pltpu.VMEM((bins, pairs), bf16),
+            pltpu.VMEM((bins, every, every), f32),
+            pltpu.VMEM((every, bins, every), f32),
+            pltpu.VMEM((1, slots), jnp.int32),
+            pltpu.SMEM((bins,), f32),
+            pltpu.VMEM((3, 1, slots), jnp.int32),
+            pltpu.SMEM((3, 1, slots), jnp.int32),
+            pltpu.SMEM((1, slots), jnp.int32),
             pltpu.VMEM((bins, by), f32),
-            pltpu.VMEM((every, table.shape[1]), bf16),
+            pltpu.VMEM((every, pairs), bf16),
             side, side, side, side,
             pltpu.VMEM((half, nz, bx, bins, by), bf16),
             pltpu.VMEM((n_bin, half, share, bx, bins, by), bf16),
             pltpu.VMEM((n_bin, half, share, bx, bins, by), bf16),
             pltpu.VMEM((every, by), f32),
-            pltpu.VMEM((table.shape[1], 2 * by), bf16),
+            pltpu.VMEM((pairs, 2 * by), bf16),
             third, third, third, third,
             dma((slots,)), dma((slots,)), dma((slots,)), dma((slots,)),
             dma((2, slots)), dma((2, slots)),
             dma((n_bin - 1, half)), dma((n_bin - 1, half)),
             dma((n_bin - 1, half)), dma((n_bin - 1, half)),
             dma((n_bin - 1,)), dma((n_bin - 1,)),
-            dma((half,)), dma((bins,)), dma((3,)), dma((3,)), dma(()), dma(()),
+            dma((half,)), dma((slots,)), dma((5,)), dma((3,)), dma((3,)), dma(()),
         ],
         compiler_params=pltpu.CompilerParams(collective_id=0, has_side_effects=True, vmem_limit_bytes=42 << 20),
-    )(order_rows, fall_speed, spectrum, jnp.transpose(wind, (1, 0, 2)), table)
+    )(*(pltpu.with_memory_space_constraint(a, pltpu.HBM) for a in inputs))
 
     return pl.pallas_call(
         update_body,

time: 105 us -> 98.8 us (0.941)
  local copies, waits for them, and re-layouts: 4.43 us -> 0.01 us
  other arithmetic: 1.31 us -> 0 us
    unnamed x7 -> x2, local copies, waits for them, and re-layouts: 2.77 us -> 0.01 us
where the time goes in v4:
time: 98.8 us; the launch traced here: 98.7 us
  Pallas kernels  98 us (99%)
    pallas_call x1, Pallas kernels, local(): pl.pallas_call(step_body, in_specs=[pl.BlockSpec(memory_space=pltpu.HBM)]...  94.3 us
    pallas_call x1, Pallas kernels, local(): pl.pallas_call(update_body, in_specs=[smem, smem, vmem, vmem], out_specs=...  3.74 us

profile of v4, /device:TPU:1, one launch (start us, length us, event | category | flops | bytes accessed | tf_op | source)
XLA Modules:
  0.0 98.7 jit_solution(18040051496370335237)
XLA Ops:
  0.0 0.0 copy-start
  0.7 94.3 %shard_map.64 = (f32[8,12,8,16,128]{4,3,2,1,0:T(8,128)S(1)}, bf16[4,12,8,16,128]{4,3,2,1,0:T(8,128)(2,1)S(1)}) custom-call(s32[1,8]{1,0:T(1,128)} %order_hbm.1, f32[16]{0:T(128)} %fall_hbm.1, f32[16,8,12,8,128]{4,3,2,1,0:T(8,128)} %spec_hbm.1, f32[12,8,128]{2,1,0:T(8,128)} %bitcast.5, bf16[64,16,64]{2,1,0:T(8,128)(2,1)} %bitcast.4), custom_call_target="tpu_custom_call" | custom-call | tf_op jit(solution)/shard_map/pallas_call | solution.py:430
  95.0 0.0 copy-done
  95.0 3.7 %shard_map.65 = f32[16,8,12,8,128]{4,3,2,1,0:T(8,128)} custom-call(s32[8]{0:T(128)S(1)} %bitcast.3, s32[1]{0:T(128)S(6)} %copy.7.count_ref, f32[8,12,8,16,128]{4,3,2,1,0:T(8,128)S(1)} %get-tuple-element.7.settled_ref, bf16[4,12,8,16,128]{4,3,2,1,0:T(8,128)(2,1)S(1)} %get-tuple-element.8.tend_ref), custom_call_target="tpu_custom_call" | custom-call | tf_op jit(solution)/shard_map/pallas_call | solution.py:469
Async XLA Ops:
  0.0 95.0 %copy-start = (s32[1,8]{1,0:T(1,128)S(1)}, s32[1,8]{1,0:T(1,128)}, u32[]{:S(2)}) copy-start(s32[1,8]{1,0:T(1,128)} %order_hbm.1) | copy-start | bytes 100

commit v5 on v4

--- a/solution.py
+++ b/solution.py
@@ -107,6 +107,7 @@
     right, left = lax.rem(blk + 1, n_blk), lax.rem(blk + last, n_blk)
     right2, left2 = lax.rem(blk + 2, n_blk), lax.rem(blk + last - 1, n_blk)
     sibling, across = bin_ + 1 - 2 * lax.rem(bin_, 2), lax.rem(bin_ + 2, n_bin)
+    pair = blk + 1 - 2 * lax.rem(blk, 2)
     peers = [lax.rem(bin_ + k, n_bin) for k in range(1, n_bin)]
 
     barrier = pltpu.get_barrier_semaphore()
@@ -114,7 +115,8 @@
         pl.semaphore_signal(barrier, inc=1, device_id={"blk": side}, device_id_type=MESH)
     for peer in peers:
         pl.semaphore_signal(barrier, inc=1, device_id={"bin": peer}, device_id_type=MESH)
-    pl.semaphore_wait(barrier, 4 + n_bin - 1)
+    pl.semaphore_signal(barrier, inc=1, device_id={"blk": pair, "bin": across}, device_id_type=MESH)
+    pl.semaphore_wait(barrier, 5 + n_bin - 1)
 
     row_copies = [
         pltpu.make_async_remote_copy(
@@ -141,12 +143,12 @@
 
     def table_copy(k):
         src, part, peer = (
-            (own_table_ref, table_part(bin_), sibling),
-            (own_table_ref, table_part(bin_), across),
-            (table_part(across), table_part(across), sibling),
+            (own_table_ref, table_part(bin_), {"bin": sibling}),
+            (own_table_ref, table_part(bin_), {"blk": pair, "bin": across}),
+            (table_part(across), table_part(across), {"bin": sibling}),
         )[k]
         return pltpu.make_async_remote_copy(
-            src, part, table_sent.at[k], table_got.at[k], device_id={"bin": peer}, device_id_type=MESH
+            src, part, table_sent.at[k], table_got.at[k], device_id=peer, device_id_type=MESH
         )
 
     def third_copy(r):
@@ -269,19 +271,17 @@
                 head = [third_left[row, z, first : first + 8, :].astype(f32)] + head
                 tail = tail + [third_right[g, z, first : first + 8, :].astype(f32)]
                 adv = advect_cells(head + own + tail, pos, cw * 0.5, cw * (1.0 / 6.0))
-                for x in range(bx):
-                    settled_ref[g, z, x, first : first + 8, :] = adv[x] - fall * (adv[x] - above[x])
+                settled = jnp.stack([adv[x] - fall * (adv[x] - above[x]) for x in range(bx)])
+                settled_ref[g, first : first + 8, z] = jnp.swapaxes(settled, 0, 1)
+
+                @pl.when(g < half)
+                def _():
+                    for x in range(bx):
+                        picks[g, z, x, first : first + 8, :] = settled[x].astype(bf16)
+
                 return tuple(adv)
 
             lax.fori_loop(0, nz, level, tuple(jnp.zeros((8, by), f32) for _ in range(bx)))
-
-    def pick(g):
-        def level(z, carry):
-            for x in range(bx):
-                picks[g, z, x] = settled_ref[g, z, x].astype(bf16)
-            return carry
-
-        lax.fori_loop(0, nz, level, 0)
 
     def collect(g):
         def pair(step, carry):
@@ -323,7 +323,6 @@
 
         @pl.when(g < half)
         def _():
-            pick(g)
             for copy in pick_copies(g):
                 copy.start()
             got[bin_, g] = picks[g, pl.ds(bin_ * share, share)]
@@ -377,41 +376,32 @@
 
 
 def update_body(order_ref, count_ref, settled_ref, tend_ref, out_ref, rows_ref, out_sem):
-    bins, slots, nz, bx, by = out_ref.shape
-    half = slots // 2
-
-    def copy(g):
-        return pltpu.make_async_copy(rows_ref.at[g], out_ref.at[:, order_ref[g]], out_sem.at[g])
+    slots = settled_ref.shape[0]
+    half, bins, nz, bx, by = rows_ref.shape
+
+    def copy(src, g):
+        return pltpu.make_async_copy(src.at[g], out_ref.at[:, order_ref[g]], out_sem.at[g])
+
+    for g in range(half, slots):
+        copy(settled_ref, g).start()
 
     def active(g, carry):
-        on = jnp.full((bx, bins, by), g, jnp.int32) < count_ref[0]
+        on = jnp.full((bins, bx, by), g, jnp.int32) < count_ref[0]
 
         def level(z, inner):
-            add = tend_ref[g, z].astype(f32) * time_step
-            rows_ref[g, :, z] = jnp.swapaxes(settled_ref[g, z] + jnp.where(on, add, 0.0), 0, 1)
+            add = jnp.swapaxes(tend_ref[g, z].astype(f32), 0, 1) * time_step
+            rows_ref[g, :, z] = settled_ref[g, :, z] + jnp.where(on, add, 0.0)
             return inner
 
         lax.fori_loop(0, nz, level, 0)
-        copy(g).start()
-        return carry
-
-    def idle(g, carry):
-        def level(z, inner):
-            rows_ref[g, :, z] = jnp.swapaxes(settled_ref[g, z], 0, 1)
-            return inner
-
-        lax.fori_loop(0, nz, level, 0)
-        copy(g).start()
+        copy(rows_ref, g).start()
         return carry
 
     lax.fori_loop(0, half, active, 0)
-    lax.fori_loop(half, slots, idle, 0)
-
-    def finish(g, carry):
-        copy(g).wait()
-        return carry
-
-    lax.fori_loop(0, slots, finish, 0)
+    for g in range(half):
+        copy(rows_ref, g).wait()
+    for g in range(half, slots):
+        copy(settled_ref, g).wait()
 
 
 def local(spectrum, wind, fall_speed, collection, act_order, act_count):
@@ -432,7 +422,7 @@
         in_specs=[pl.BlockSpec(memory_space=pltpu.HBM)] * 5,
         out_specs=[vmem, hbm],
         out_shape=[
-            jax.ShapeDtypeStruct((slots, nz, bx, bins, by), f32),
+            jax.ShapeDtypeStruct((slots, bins, nz, bx, by), f32),
             jax.ShapeDtypeStruct((half, nz, bx, bins, by), bf16),
         ],
         scratch_shapes=[
@@ -471,7 +461,7 @@
         in_specs=[smem, smem, vmem, vmem],
         out_specs=hbm,
         out_shape=jax.ShapeDtypeStruct(spectrum.shape, f32),
-        scratch_shapes=[pltpu.VMEM((slots, bins, nz, bx, by), f32), dma((slots,))],
+        scratch_shapes=[pltpu.VMEM((half, bins, nz, bx, by), f32), dma((slots,))],
         compiler_params=pltpu.CompilerParams(vmem_limit_bytes=16 << 20),
     )(order, act_count, settled, back)
 

time: 98.8 us -> 97.2 us (0.984)
  Pallas kernels: 98 us -> 96.5 us
    pallas_call x1, Pallas kernels: 94.3 us -> 93.2 us  [local(): pl.pallas_call(step_body, in_specs=[pl.BlockSpec(memory_space=pltpu.HBM)]...]
where the time goes in v5:
time: 97.2 us
  Pallas kernels  96.5 us (99%)
    pallas_call x1, Pallas kernels, local(): pl.pallas_call(step_body, in_specs=[pl.BlockSpec(memory_space=pltpu.HBM)]...  93.2 us
    pallas_call x1, Pallas kernels, local(): pl.pallas_call(update_body, in_specs=[smem, smem, vmem, vmem], out_specs=...  3.29 us

profile of v5, /device:TPU:1, one launch (start us, length us, event | category | flops | bytes accessed | tf_op | source)
XLA Modules:
  0.0 97.2 jit_solution(11182070207943112602)
XLA Ops:
  0.0 0.0 copy-start
  0.7 93.2 %shard_map.64 = (f32[8,16,12,8,128]{4,3,2,1,0:T(8,128)S(1)}, bf16[4,12,8,16,128]{4,3,2,1,0:T(8,128)(2,1)S(1)}) custom-call(s32[1,8]{1,0:T(1,128)} %order_hbm.1, f32[16]{0:T(128)} %fall_hbm.1, f32[16,8,12,8,128]{4,3,2,1,0:T(8,128)} %spec_hbm.1, f32[12,8,128]{2,1,0:T(8,128)} %bitcast.5, bf16[64,16,64]{2,1,0:T(8,128)(2,1)} %bitcast.4), custom_call_target="tpu_custom_call" | custom-call | tf_op jit(solution)/shard_map/pallas_call | solution.py:420
  93.9 0.0 copy-done
  93.9 3.3 %shard_map.65 = f32[16,8,12,8,128]{4,3,2,1,0:T(8,128)} custom-call(s32[8]{0:T(128)S(1)} %bitcast.3, s32[1]{0:T(128)S(6)} %copy.7.count_ref, f32[8,16,12,8,128]{4,3,2,1,0:T(8,128)S(1)} %get-tuple-element.7.settled_ref, bf16[4,12,8,16,128]{4,3,2,1,0:T(8,128)(2,1)S(1)} %get-tuple-element.8.tend_ref), custom_call_target="tpu_custom_call" | custom-call | tf_op jit(solution)/shard_map/pallas_call | solution.py:459
Async XLA Ops:
  0.0 93.9 %copy-start = (s32[1,8]{1,0:T(1,128)S(1)}, s32[1,8]{1,0:T(1,128)}, u32[]{:S(2)}) copy-start(s32[1,8]{1,0:T(1,128)} %order_hbm.1) | copy-start | bytes 100

commit v6 on v5

--- a/solution.py
+++ b/solution.py
@@ -84,6 +84,7 @@
 ):
     bins, slots, nz, bx, by = spec_hbm.shape
     half = slots // 2
+    ahead = half - 1
     flat = pieces(spec_ref)
     small_copies = [
         pltpu.make_async_copy(src, dst, small_sem.at[k])
@@ -228,7 +229,7 @@
     orders_copy = pltpu.make_async_copy(rows_got, orders, orders_sem)
     orders_copy.start()
     orders_copy.wait()
-    lax.fori_loop(0, half, pack_and_send, 0)
+    lax.fori_loop(0, ahead, pack_and_send, 0)
     for b in range(bins):
         fall_ref[b : b + 1, :] = jnp.full((1, by), fall_speed_ref[b], f32) * courant
     small_copies[4].wait()
@@ -241,7 +242,7 @@
         pack(g)
         return carry
 
-    lax.fori_loop(half, slots, pack_later, 0)
+    lax.fori_loop(ahead, slots, pack_later, 0)
 
     def third_arrived(r, carry):
         third_copy(r).wait_recv()
@@ -326,7 +327,10 @@
             for copy in pick_copies(g):
                 copy.start()
             got[bin_, g] = picks[g, pl.ds(bin_ * share, share)]
-            for copy in halos(g + half):
+
+        @pl.when(g + ahead < slots)
+        def _():
+            for copy in halos(g + ahead):
                 copy.start()
 
         @pl.when(g == 0)

time: 97.2 us -> 95.1 us (0.978)
  Pallas kernels: 96.5 us -> 94.3 us
    pallas_call x1, Pallas kernels: 93.2 us -> 91 us  [local(): pl.pallas_call(step_body, in_specs=[pl.BlockSpec(memory_space=pltpu.HBM)]...]
where the time goes in v6:
time: 95.1 us; the launch traced here: 95 us
  Pallas kernels  94.3 us (99%)
    pallas_call x1, Pallas kernels, local(): pl.pallas_call(step_body, in_specs=[pl.BlockSpec(memory_space=pltpu.HBM)]...  91 us
    pallas_call x1, Pallas kernels, local(): pl.pallas_call(update_body, in_specs=[smem, smem, vmem, vmem], out_specs=...  3.29 us

profile of v6, /device:TPU:1, one launch (start us, length us, event | category | flops | bytes accessed | tf_op | source)
XLA Modules:
  0.0 95.0 jit_solution(16981742376214590796)
XLA Ops:
  0.0 0.0 copy-start
  0.7 91.0 %shard_map.64 = (f32[8,16,12,8,128]{4,3,2,1,0:T(8,128)S(1)}, bf16[4,12,8,16,128]{4,3,2,1,0:T(8,128)(2,1)S(1)}) custom-call(s32[1,8]{1,0:T(1,128)} %order_hbm.1, f32[16]{0:T(128)} %fall_hbm.1, f32[16,8,12,8,128]{4,3,2,1,0:T(8,128)} %spec_hbm.1, f32[12,8,128]{2,1,0:T(8,128)} %bitcast.5, bf16[64,16,64]{2,1,0:T(8,128)(2,1)} %bitcast.4), custom_call_target="tpu_custom_call" | custom-call | tf_op jit(solution)/shard_map/pallas_call | solution.py:424
  91.7 0.0 copy-done
  91.7 3.3 %shard_map.65 = f32[16,8,12,8,128]{4,3,2,1,0:T(8,128)} custom-call(s32[8]{0:T(128)S(1)} %bitcast.3, s32[1]{0:T(128)S(6)} %copy.7.count_ref, f32[8,16,12,8,128]{4,3,2,1,0:T(8,128)S(1)} %get-tuple-element.7.settled_ref, bf16[4,12,8,16,128]{4,3,2,1,0:T(8,128)(2,1)S(1)} %get-tuple-element.8.tend_ref), custom_call_target="tpu_custom_call" | custom-call | tf_op jit(solution)/shard_map/pallas_call | solution.py:463
Async XLA Ops:
  0.0 91.7 %copy-start = (s32[1,8]{1,0:T(1,128)S(1)}, s32[1,8]{1,0:T(1,128)}, u32[]{:S(2)}) copy-start(s32[1,8]{1,0:T(1,128)} %order_hbm.1) | copy-start | bytes 100
